TPU v7x, 256 devices: a whole 4x4x8 slice. The times are simulated.
256 devices in a mesh: win: 32 (over z, y_lo, core), chan: 8 (over x, y_hi).
Axes of the slice: x: 4, y: 4 (y_hi: 2, y_lo: 2; y = y_hi * 2 + y_lo), z: 8, core: 2. Of those that a mesh axis runs over, the one named last changes fastest.
Arguments:
- traces: bfloat16 [256, 1024, 4096], P('win', 'chan'), may hold values from -6 to 6
- source_block: int32 [3], replicated, may hold values from 0 to 7, as said below
- pair_source: int32 [3, 4096], P(None, 'chan'), may hold values from 0 to 127
- pair_receiver: int32 [3, 4096], P(None, 'chan'), may hold values from 0 to 127
- pair_bin: int32 [3, 4096], P(None, 'chan'), may hold values from 0 to 1023, as said below
- bin_slot: int32 [1024], replicated, may hold values from 0 to 1023, as said below
Outputs:
- stacks: float32 [3, 4096, 1024], P(None, 'win', 'chan')
Inputs may be any that keep to these rules, and one draw needn't show every extreme that they name: `source_block`: not every step names the same block; some step names block 0 and some step block 8 - 1. `pair_bin`: among the 512 pairs of one index of chan in a step, at most 128 have bins with bin_slot // 128 equal to one owner; in every step one owner gets exactly 128 from every index of chan. `bin_slot`: each bin has its own row.
All inputs are finite; a program needn't handle non-finite values.
Results may differ from a plain program's by a relative error of at most 0.0056.
Values may be sent and summed in bfloat16 or wider, within the bound.
No kernel may reach another device: no remote copies, remote signals or barrier semaphores. Data moves between devices by JAX's collectives and lax.ppermute only.
A program may use at most 64 MiB of HBM per device.

v0:
```python
import math

import jax
import jax.numpy as jnp
from jax import lax
from jax.sharding import PartitionSpec as P

WLEN = 4096
F = 128
FREQ0 = 256
LAGS = 4096
BIN_DEV = 128
STEPS = 3
P_DEV = 512


def from_root(block, axis, holder):
    block = jnp.where(lax.axis_index(axis) == holder, block, jnp.zeros_like(block))
    return lax.psum(block, axis)


def forward_table():
    samples = jnp.arange(WLEN, dtype=jnp.int32)
    freq_ids = FREQ0 + jnp.arange(F, dtype=jnp.int32)
    phases = samples[:, None] * freq_ids[None, :] % WLEN
    angles = phases.astype(jnp.float32) * (2.0 * math.pi / WLEN)
    return jnp.concatenate([jnp.cos(angles), -jnp.sin(angles)], axis=1).astype(jnp.bfloat16)


def lag_table(length, norm_scale):
    samples = jnp.arange(length, dtype=jnp.int32)
    freq_ids = FREQ0 + jnp.arange(F, dtype=jnp.int32)
    phases = freq_ids[:, None] * (samples[None, :] + (WLEN - LAGS // 2)) % WLEN
    angles = phases.astype(jnp.float32) * (2.0 * math.pi / WLEN)
    return jnp.concatenate([jnp.cos(angles), -jnp.sin(angles)], axis=0) * norm_scale


def cross_spectra(src_spec, rec_spec):
    src_re, src_im = (src_spec[..., :F], src_spec[..., F:])
    rec_re, rec_im = (rec_spec[..., :F], rec_spec[..., F:])
    real_part = jnp.sum(src_re * rec_re + src_im * rec_im, axis=0)
    imag_part = jnp.sum(src_re * rec_im - src_im * rec_re, axis=0)
    return jnp.concatenate([real_part, imag_part], axis=-1)


def project_lags(lag_basis, binned):
    return lax.dot_general(
        lag_basis, binned, (((0,), (1,)), ((), ())), precision=lax.Precision.HIGHEST
    )


def pick_channels(block, picks):
    chooser = (picks[:, None] == jnp.arange(block.shape[1], dtype=jnp.int32)[None, :]).astype(
        jnp.bfloat16
    )
    return jnp.einsum("pc,wcf->wpf", chooser, block, preferred_element_type=jnp.float32)


def on_device(traces, source_block, pair_source, pair_receiver, pair_bin, bin_slot):
    win_local, chan_local, samples_count = traces.shape
    chan_count = lax.axis_size("chan")
    win_count = lax.axis_size("win")
    lag_count = LAGS // win_count
    norm_scale = 1.0 / math.sqrt(2.0 * F * win_count * win_local)
    capacity = min(2 * P_DEV // chan_count, 3 * P_DEV // 4)
    spectra = jnp.dot(
        traces.reshape(win_local * chan_local, samples_count),
        forward_table(),
        preferred_element_type=jnp.float32,
    )
    power = jnp.mean(spectra * spectra, axis=-1, keepdims=True)
    whitened = (
        (spectra * lax.rsqrt(power + 1e-06))
        .astype(jnp.bfloat16)
        .reshape(win_local, chan_local, 2 * F)
    )
    bin_range = jnp.arange(bin_slot.shape[0], dtype=jnp.int32)
    pair_range = jnp.arange(P_DEV, dtype=jnp.int32)
    lower_tri = (pair_range[None, :] <= pair_range[:, None]).astype(jnp.bfloat16)
    results = []
    for section_index in range(STEPS):
        source = from_root(whitened, "chan", source_block[section_index])
        src_spec = pick_channels(source, pair_source[section_index])
        rec_spec = pick_channels(whitened, pair_receiver[section_index])
        partial_value = cross_spectra(src_spec, rec_spec).astype(jnp.bfloat16)
        matches_bin = pair_bin[section_index][:, None] == bin_range[None, :]
        slot_ids = jnp.sum(jnp.where(matches_bin, bin_slot[None, :], 0), axis=1)
        owners = slot_ids // BIN_DEV
        row_in_owner = slot_ids % BIN_DEV
        matches = owners[:, None] == jnp.arange(chan_count, dtype=jnp.int32)[None, :]
        running = jnp.dot(
            lower_tri, matches.astype(jnp.bfloat16), preferred_element_type=jnp.float32
        ).astype(jnp.int32)
        position = jnp.sum(jnp.where(matches, running - 1, 0), axis=1)
        target = owners * capacity + position
        slot_range = jnp.arange(chan_count * capacity, dtype=jnp.int32)
        placed = slot_range[:, None] == target[None, :]
        outgoing = jnp.dot(
            placed.astype(jnp.bfloat16), partial_value, preferred_element_type=jnp.float32
        )
        outgoing = outgoing.astype(jnp.bfloat16).reshape(chan_count, capacity, 2 * F)
        labels = jnp.sum(jnp.where(placed, row_in_owner[None, :] + 1, 0), axis=1) - 1
        labels = labels.reshape(chan_count, capacity)
        incoming, received_rows = (
            lax.all_to_all(outgoing, "chan", split_axis=0, concat_axis=0, tiled=True),
            lax.all_to_all(labels, "chan", split_axis=0, concat_axis=0, tiled=True),
        )
        onehot = (
            received_rows.reshape(-1)[None, :] == jnp.arange(BIN_DEV, dtype=jnp.int32)[:, None]
        ).astype(jnp.bfloat16)
        binned = jnp.dot(onehot, incoming.reshape(-1, 2 * F), preferred_element_type=jnp.float32)
        stacked = lax.psum_scatter(
            project_lags(lag_table(lag_count * lax.axis_size("win"), norm_scale), binned),
            "win",
            scatter_dimension=0,
            tiled=True,
        )
        results.append(stacked)
    return jnp.stack(results)


def solution(mesh):
    placed = (P("win", "chan", None), P(), P(None, "chan"), P(None, "chan"), P(None, "chan"), P())
    return jax.shard_map(
        on_device, mesh=mesh, in_specs=placed, out_specs=P(None, "win", "chan"), check_vma=False
    )
```

profile of v0, /device:TPU:1, one launch (start us, length us, event | category | flops | bytes accessed | tf_op | source)
XLA Modules:
  0.0 525.5 jit_solution(2868573302361774314)
XLA Ops:
  6.5 8.6 %cosine_convert_fusion = (bf16[4096,128]{1,0:T(8,128)(2,1)S(1)}, bf16[4096,128]{1,0:T(8,128)(2,1)S(1)}) fusion(s32[128]{0:T(128)S(1)} %iota_add_fusion.1), kind=kLoop, calls=%fused_computation.45 | loop fusion | flops 8912896 | bytes 2097664 | tf_op jit(solution)/shard_map/convert.6
  15.1 5.8 %multiply_reduce_fusion = (f32[1024]{0:T(1024)S(1)}, f32[256,1024]{1,0:T(8,128)S(1)}) fusion(bf16[1024,4096]{1,0:T(8,128)(2,1)} %bitcast.102, bf16[4096,128]{1,0:T(8,128)(2,1)S(1)} %get-tuple-element.41, bf16[4096,128]{1,0:T(8,128)(2,1)S(1)} %get-tuple-element.40), kind=kOutput, calls=%fused_computation.76 | convolution fusion | flops 2152201216 | bytes 11538432 | tf_op jit(solution)/shard_map/dot_general | solution.py:66
  21.0 0.7 fusion.100
  23.6 1.4 bitcast_select_fusion.2
  25.0 1.2 select_reduce_fusion.5
  27.4 7.5 %all-to-all-start = ((s32[8,1,128]{2,1,0:T(1,128)}), s32[8,1,128]{2,1,0:T(1,128)S(1)}, u32[]{:S(2)}, u32[]{:S(2)}) async-start(s32[8,1,128]{2,1,0:T(1,128)} %bitcast.1), calls=%async_computation | async-start | bytes 8192 | tf_op jit(solution)/shard_map/all_to_all | solution.py:106
  35.1 2.7 convolution_bitcast_fusion.4
  37.8 91.2 %all-reduce.3.cloned.1.call-done = (bf16[8,128,256]{1,2,0:T(8,128)(2,1)}, bf16[8,128,256]{1,2,0:T(8,128)(2,1)}, bf16[8,128,256]{1,2,0:T(8,128)(2,1)}) async-done(((bf16[8,128,256]{1,2,0:T(8,128)(2,1)}, bf16[8,128,256]{1,2,0:T(8,128)(2,1)}, bf16[8,128,256]{1,2,0:T(8,128)(2,1)}), (bf16[8,128,256]{1,2,0:T(8,128)(2,1)}, bf16[8,128,256]{1,2,0:T(8,128)(2,1)}, ...) | async-done | bytes 1572880 | tf_op jit(solution)/shard_map/psum | solution.py:19
  129.0 2.0 convolution_bitcast_fusion.5
  131.4 1.1 add_reduce_fusion.2
  132.5 1.3 fusion.22
  133.8 4.0 all-to-all-start.1
  138.0 9.4 %fusion.37 = (f32[128,4096]{1,0:T(8,128)S(1)}, f32[128,4096]{1,0:T(8,128)}) fusion(s32[4096]{0:T(1024)S(1)} %iota_add_fusion, s32[128]{0:T(128)S(1)} %iota_add_fusion.1), kind=kLoop, calls=%fused_computation.79 | loop fusion | flops 7864320 | bytes 4211200 | tf_op jit(solution)/shard_map/cos | solution.py:35
  147.6 9.6 %fusion.2 = f32[4096,128]{1,0:T(8,128)} fusion(f32[128,256]{1,0:T(8,128)S(1)} %fusion.42, f32[128,4096]{1,0:T(8,128)} %get-tuple-element.21, f32[128,4096]{1,0:T(8,128)S(1)} %get-tuple-element.20), kind=kOutput, calls=%fused_computation.11 | convolution fusion | flops 1612709888 | bytes 6422528 | tf_op jit(solution)/shard_map/dot_general | solution.py:47
  158.4 6.6 %all-to-all-start.2 = ((s32[8,1,128]{2,1,0:T(1,128)}), s32[8,1,128]{2,1,0:T(1,128)S(1)}, u32[]{:S(2)}, u32[]{:S(2)}) async-start(s32[8,1,128]{2,1,0:T(1,128)} %bitcast.16), calls=%async_computation.3 | async-start | bytes 8192 | tf_op jit(solution)/shard_map/all_to_all | solution.py:106
  165.3 0.8 convolution_bitcast_fusion.2
  166.3 0.8 convolution_bitcast_fusion.3
  167.1 1.1 add_reduce_fusion.1
  168.7 2.7 all-to-all-done.2
  171.4 12.4 %all_to_all.33 = bf16[8,128,256]{2,1,0:T(8,128)(2,1)S(1)} all-to-all(bf16[8,128,256]{2,1,0:T(8,128)(2,1)S(1)} %bitcast.85), channel_id=1, replica_groups=mesh['win'=32,'chan'=8] {'chan'}, dimensions={0} | all-to-all | bytes 1048576 | tf_op jit(solution)/shard_map/all_to_all | solution.py:105
  184.1 9.6 %fusion.1 = f32[4096,128]{1,0:T(8,128)} fusion(f32[128,256]{1,0:T(8,128)S(1)} %fusion.43, f32[128,4096]{1,0:T(8,128)} %get-tuple-element.21, f32[128,4096]{1,0:T(8,128)S(1)} %get-tuple-element.20), kind=kOutput, calls=%fused_computation.10 | convolution fusion | flops 1612709888 | bytes 6422528 | tf_op jit(solution)/shard_map/dot_general | solution.py:47
  194.9 3.4 all-to-all-start.4
  198.6 0.8 convolution_bitcast_fusion
  199.7 0.8 convolution_bitcast_fusion.1
  200.5 1.1 add_reduce_fusion
  202.1 2.7 all-to-all-done.4
  204.8 12.4 %all_to_all.34 = bf16[8,128,256]{2,1,0:T(8,128)(2,1)S(1)} all-to-all(bf16[8,128,256]{2,1,0:T(8,128)(2,1)S(1)} %bitcast.86), channel_id=1, replica_groups=mesh['win'=32,'chan'=8] {'chan'}, dimensions={0} | all-to-all | bytes 1048576 | tf_op jit(solution)/shard_map/all_to_all | solution.py:105
  217.4 9.6 %fusion = f32[4096,128]{1,0:T(8,128)} fusion(f32[128,256]{1,0:T(8,128)S(1)} %fusion.44, f32[128,4096]{1,0:T(8,128)} %get-tuple-element.21, f32[128,4096]{1,0:T(8,128)S(1)} %get-tuple-element.20), kind=kOutput, calls=%fused_computation.9 | convolution fusion | flops 1612709888 | bytes 6422528 | tf_op jit(solution)/shard_map/dot_general | solution.py:47
  227.1 52.3 %reduce-scatter.4.cloned.1.call-done = f32[128,128]{1,0:T(8,128)} async-done(((f32[4096,128]{1,0:T(8,128)}), f32[128,128]{1,0:T(8,128)}) %reduce-scatter.4.cloned.1.call-update) | async-done | bytes 65552 | tf_op jit(solution)/shard_map/reduce_scatter | solution.py:112
  279.4 118.7 %reduce-scatter.6.cloned.1.call-done = f32[128,128]{1,0:T(8,128)} async-done(((f32[4096,128]{1,0:T(8,128)}), f32[128,128]{1,0:T(8,128)}) %reduce-scatter.6.cloned.1.call-update) | async-done | bytes 65552 | tf_op jit(solution)/shard_map/reduce_scatter | solution.py:112
  398.1 118.8 %reduce-scatter.8.cloned.1.call-done = f32[128,128]{1,0:T(8,128)} async-done(((f32[4096,128]{1,0:T(8,128)}), f32[128,128]{1,0:T(8,128)}) %reduce-scatter.8.cloned.1.call-update) | async-done | bytes 65552 | tf_op jit(solution)/shard_map/reduce_scatter | solution.py:112
  516.9 1.6 pad_maximum_fusion
  (52 shorter events, 7.0 us)
Async XLA Ops:
  6.5 122.5 %all-reduce.3.cloned.1.call-start = ((), (), s32[]{:S(2)}) async-start(), calls=%async_computation.12 | async-start | bytes 3145728 | tf_op jit(solution)/shard_map/psum | solution.py:19
  15.1 5.8 %copy-start.6 = (s32[3]{0:T(128)S(1)}, s32[3]{0:T(128)}, u32[]{:S(2)}) copy-start(s32[3]{0:T(128)} %param.7) | copy-start | bytes 40
  23.5 1.5 copy-start.3
  23.5 1.5 copy-start.7
  23.5 11.3 %copy-start.4 = (s32[3,512]{1,0:T(4,128)S(1)}, s32[3,512]{1,0:T(4,128)}, u32[]{:S(2)}) copy-start(s32[3,512]{1,0:T(4,128)} %param.8) | copy-start | bytes 18436
  23.6 11.4 %copy-start.5 = (s32[3,512]{1,0:T(4,128)S(1)}, s32[3,512]{1,0:T(4,128)}, u32[]{:S(2)}) copy-start(s32[3,512]{1,0:T(4,128)} %param.9) | copy-start | bytes 18436
  27.4 106.4 %all-to-all-start = ((s32[8,1,128]{2,1,0:T(1,128)}), s32[8,1,128]{2,1,0:T(1,128)S(1)}, u32[]{:S(2)}, u32[]{:S(2)}) async-start(s32[8,1,128]{2,1,0:T(1,128)} %bitcast.1), calls=%async_computation | async-start | bytes 8192 | tf_op jit(solution)/shard_map/all_to_all | solution.py:106
  129.0 2.3 copy-start
  133.8 13.6 %all-to-all-start.1 = ((bf16[8,128,256]{2,1,0:T(8,128)(2,1)}), bf16[8,128,256]{2,1,0:T(8,128)(2,1)S(1)}, u32[]{:S(2)}, u32[]{:S(2)}) async-start(bf16[8,128,256]{2,1,0:T(8,128)(2,1)} %bitcast.12), calls=%async_computation.1 | async-start | bytes 1048576 | tf_op jit(solution)/shard_map/all_to_all | solution.py:105
  137.8 141.6 %reduce-scatter.4.cloned.1.call-start = ((), (), s32[]{:S(2)}) async-start(), calls=%async_computation.9 | async-start | bytes 2162688 | tf_op jit(solution)/shard_map/reduce_scatter | solution.py:112
  158.4 13.0 %all-to-all-start.2 = ((s32[8,1,128]{2,1,0:T(1,128)}), s32[8,1,128]{2,1,0:T(1,128)S(1)}, u32[]{:S(2)}, u32[]{:S(2)}) async-start(s32[8,1,128]{2,1,0:T(1,128)} %bitcast.16), calls=%async_computation.3 | async-start | bytes 8192 | tf_op jit(solution)/shard_map/all_to_all | solution.py:106
  165.0 233.1 %reduce-scatter.6.cloned.1.call-start = ((), (), s32[]{:S(2)}) async-start(), calls=%async_computation.10 | async-start | bytes 2162688 | tf_op jit(solution)/shard_map/reduce_scatter | solution.py:112
  165.3 1.0 copy-start.2
  194.9 9.9 %all-to-all-start.4 = ((s32[8,1,128]{2,1,0:T(1,128)}), s32[8,1,128]{2,1,0:T(1,128)S(1)}, u32[]{:S(2)}, u32[]{:S(2)}) async-start(s32[8,1,128]{2,1,0:T(1,128)} %bitcast.29), calls=%async_computation.6 | async-start | bytes 8192 | tf_op jit(solution)/shard_map/all_to_all | solution.py:106
  198.3 318.6 %reduce-scatter.8.cloned.1.call-start = ((), (), s32[]{:S(2)}) async-start(), calls=%async_computation.11 | async-start | bytes 2162688 | tf_op jit(solution)/shard_map/reduce_scatter | solution.py:112
  198.6 1.0 copy-start.1
Sparse Core Ops, SparseCore 0:
  25.1 103.8 all-reduce.2
  157.3 121.9 reduce-scatter.3
  282.0 115.9 reduce-scatter.5
  400.4 116.3 reduce-scatter.7
where the time goes:
time: 536 us; the launch traced here: 525 us
  waiting for transfers between devices  386 us (72%)
  matrix products  46.5 us (9%)
  other arithmetic  28.2 us (5%)
  blocking collectives  24.8 us (5%)
  starting transfers between devices  22.2 us (4%)
  between operations  15.7 us (3%)
    reduce_scatter x3, waiting for transfers between devices, on_device(): lax.psum_scatter(project_lags(lag_table(lag_count * lax.axis_size('win'),...  290 us
    psum x1, waiting for transfers between devices, from_root(): return lax.psum(block, axis)  91.2 us
    dot_general x3, matrix products, project_lags(): lax.dot_general(lag_basis, binned, (((0,), (1,)), ((), ())), precision=la...  28.9 us
    all_to_all x2, blocking collectives, on_device(): lax.all_to_all(outgoing, 'chan', split_axis=0, concat_axis=0, tiled=True)  24.8 us
    all_to_all x3, starting transfers between devices, on_device(): lax.all_to_all(labels, 'chan', split_axis=0, concat_axis=0, tiled=True)  17.5 us
  transfers between devices with their start and end apart: 8, of which 6 were waited for; matrix products, arithmetic and copies ran while one was open for 9% of the time, Pallas kernels for 0%

commit v1 on v0

v1 whole, which is shorter than its diff:
```python
import math

import jax
import jax.numpy as jnp
import numpy as np
from jax import lax
from jax.experimental import pallas as pl
from jax.experimental.pallas import tpu as pltpu
from jax.sharding import PartitionSpec as P

WLEN = 4096
F = 128
FREQ0 = 256
LAGS = 4096
CH_DEV = 128
BIN_DEV = 128
STEPS = 3
WIN_DEV = 8
P_DEV = 512
BINS = 1024
N_WIN = 32
N_CHAN = 8

FG = F // N_CHAN
COLS = 2 * FG
ROWS = WIN_DEV * COLS
QUARTERS = P_DEV // 128
META = STEPS * 4 * QUARTERS
SUB = BIN_DEV // N_WIN
PART = STEPS * SUB
NT = (((1,), (1,)), ((), ()))
BF = jnp.bfloat16
F32 = jnp.float32


def column_order():
    group, part, freq = np.meshgrid(
        np.arange(N_CHAN), np.arange(2), np.arange(FG), indexing="ij"
    )
    return (part * F + group * FG + freq).reshape(-1)


def forward_rows():
    phases = (FREQ0 + np.arange(F))[:, None] * np.arange(WLEN)[None, :] % WLEN
    angles = phases.astype(np.float32) * np.float32(2.0 * math.pi / WLEN)
    rows = np.concatenate([np.cos(angles), -np.sin(angles)], axis=0)[column_order()]
    return rows.astype(BF)


def lag_rows(first_lag):
    lags = first_lag + jnp.arange(LAGS // N_WIN, dtype=jnp.int32)
    order = column_order()
    freq_ids = jnp.asarray(FREQ0 + order % F, jnp.int32)
    is_sin = jnp.asarray(order >= F)
    phases = freq_ids[None, :] * (lags[:, None] + (WLEN - LAGS // 2)) % WLEN
    angles = phases.astype(F32) * (2.0 * math.pi / WLEN)
    norm_scale = 1.0 / math.sqrt(2.0 * F * N_WIN * WIN_DEV)
    return jnp.where(is_sin[None, :], -jnp.sin(angles), jnp.cos(angles)) * norm_scale


def whiten_kernel(x_ref, table_ref, slot_ref, source_ref, receiver_ref, bin_ref, out_ref):
    step = pl.program_id(0)
    rows = x_ref[...].reshape(2 * CH_DEV, WLEN)
    spectra = lax.dot_general(table_ref[...], rows, NT, preferred_element_type=F32)
    power = jnp.sum(spectra * spectra, axis=0, keepdims=True) * (1.0 / (2 * F))
    whitened = (spectra * lax.rsqrt(power + 1e-06)).astype(BF)
    for half in range(2):
        first = pl.multiple_of((2 * step + half) * COLS, COLS)
        for group in range(N_CHAN):
            out_ref[group, pl.ds(first, COLS), :] = whitened[
                group * COLS : (group + 1) * COLS, half * CH_DEV : (half + 1) * CH_DEV
            ]

    @pl.when(step < STEPS)
    def _():
        bins = bin_ref[0]
        chosen = lax.broadcasted_iota(jnp.int32, (BINS, P_DEV), 0) == bins
        slots = jnp.sum(jnp.where(chosen, slot_ref[...], 0), axis=0, keepdims=True)
        owner = slots // BIN_DEV
        low = slots % BIN_DEV
        target = low // SUB * N_CHAN + owner
        lists = [source_ref[0], receiver_ref[0], target, low % SUB]
        block = jnp.concatenate(
            [v[:, q * 128 : (q + 1) * 128] for v in lists for q in range(QUARTERS)], axis=0
        )
        block = block.astype(F32).astype(BF)
        first = pl.multiple_of(ROWS + step * 16, 16)
        for group in range(N_CHAN):
            out_ref[group, pl.ds(first, 16), :] = block


def whiten(traces, pair_source, pair_receiver, pair_bin, bin_slot):
    lists = pl.BlockSpec((1, 1, P_DEV), lambda i: (jnp.minimum(i, STEPS - 1), 0, 0))
    return pl.pallas_call(
        whiten_kernel,
        grid=(WIN_DEV // 2,),
        in_specs=[
            pl.BlockSpec((2, CH_DEV, WLEN), lambda i: (i, 0, 0)),
            pl.BlockSpec((2 * F, WLEN), lambda i: (0, 0), pipeline_mode=pl.Buffered(1)),
            pl.BlockSpec((BINS, 1), lambda i: (0, 0), pipeline_mode=pl.Buffered(1)),
            lists,
            lists,
            lists,
        ],
        out_specs=pl.BlockSpec((N_CHAN, ROWS + META, CH_DEV), lambda i: (0, 0, 0)),
        out_shape=jax.ShapeDtypeStruct((N_CHAN, ROWS + META, CH_DEV), BF),
        compiler_params=pltpu.CompilerParams(vmem_limit_bytes=40 << 20),
    )(
        traces,
        jnp.asarray(forward_rows()),
        bin_slot.reshape(BINS, 1),
        pair_source.reshape(STEPS, 1, P_DEV),
        pair_receiver.reshape(STEPS, 1, P_DEV),
        pair_bin.reshape(STEPS, 1, P_DEV),
    )


def spread(row, count):
    index = lax.broadcasted_iota(jnp.int32, (count, row.shape[1]), 0).astype(F32)
    return jnp.where(index == row, 1.0, 0.0).astype(BF)


def pairs_kernel(block_ref, y_ref, out_ref, acc_ref):
    for s in range(STEPS):
        acc_ref[...] = jnp.zeros_like(acc_ref)
        source = y_ref[block_ref[s], :ROWS, :]

        def body(c, carry):
            lists = y_ref[c, pl.ds(ROWS + s * 16, 16), :].astype(F32)

            def row(kind):
                return jnp.concatenate(
                    [lists[kind * QUARTERS + q : kind * QUARTERS + q + 1] for q in range(QUARTERS)],
                    axis=1,
                )

            a = jnp.dot(source, spread(row(0), CH_DEV), preferred_element_type=F32)
            b = jnp.dot(
                y_ref[c, :ROWS, :], spread(row(1), CH_DEV), preferred_element_type=F32
            )
            real_part = jnp.zeros((FG, P_DEV), F32)
            imag_part = jnp.zeros((FG, P_DEV), F32)
            for w in range(WIN_DEV):
                a_re, a_im = a[w * COLS : w * COLS + FG], a[w * COLS + FG : (w + 1) * COLS]
                b_re, b_im = b[w * COLS : w * COLS + FG], b[w * COLS + FG : (w + 1) * COLS]
                real_part += a_re * b_re + a_im * b_im
                imag_part += a_re * b_im - a_im * b_re
            partial = jnp.concatenate([real_part, imag_part], axis=0)
            low = row(3)
            placed = jnp.concatenate(
                [jnp.where(low == float(k), partial, 0.0) for k in range(SUB)], axis=0
            ).astype(BF)
            acc_ref[...] += lax.dot_general(
                spread(row(2), N_WIN * N_CHAN), placed, NT, preferred_element_type=F32
            )
            return carry

        lax.fori_loop(0, N_CHAN, body, 0)
        out_ref[:, s * 128 : (s + 1) * 128] = acc_ref[...].astype(BF)


def bin_pairs(source_block, blocks):
    return pl.pallas_call(
        pairs_kernel,
        in_specs=[
            pl.BlockSpec(memory_space=pltpu.SMEM),
            pl.BlockSpec(memory_space=pltpu.VMEM),
        ],
        out_specs=pl.BlockSpec(memory_space=pltpu.VMEM),
        out_shape=jax.ShapeDtypeStruct((N_WIN * N_CHAN, STEPS * SUB * COLS), BF),
        scratch_shapes=[pltpu.VMEM((N_WIN * N_CHAN, SUB * COLS), F32)],
        compiler_params=pltpu.CompilerParams(vmem_limit_bytes=32 << 20),
    )(source_block, blocks)


def on_device(traces, source_block, pair_source, pair_receiver, pair_bin, bin_slot):
    blocks = whiten(traces, pair_source, pair_receiver, pair_bin, bin_slot)
    blocks = lax.all_to_all(blocks, "chan", 0, 0, tiled=True)
    binned = bin_pairs(source_block, blocks)
    binned = binned.reshape(N_WIN * N_CHAN, STEPS, SUB * COLS)
    binned = lax.all_to_all(binned, ("win", "chan"), 0, 0, tiled=True)
    total = jnp.sum(
        binned.reshape(N_WIN, N_CHAN, STEPS, SUB, COLS).astype(F32), axis=0
    )
    total = total.transpose(1, 2, 0, 3).reshape(PART, 2 * F).astype(BF)
    total = jnp.broadcast_to(total[None], (N_WIN, PART, 2 * F))
    total = lax.all_to_all(total, "win", 0, 0, tiled=True)
    total = total.reshape(N_WIN, STEPS, SUB, 2 * F).transpose(1, 0, 2, 3)
    total = total.reshape(STEPS, BIN_DEV, 2 * F).astype(F32)
    basis = lag_rows(lax.axis_index("win") * (LAGS // N_WIN))
    return jnp.einsum("tj,sbj->stb", basis, total, precision=lax.Precision.HIGHEST)


def solution(mesh):
    placed = (P("win", "chan", None), P(), P(None, "chan"), P(None, "chan"), P(None, "chan"), P())
    return jax.shard_map(
        on_device, mesh=mesh, in_specs=placed, out_specs=P(None, "win", "chan"), check_vma=False
    )
```

time: 536 us -> 91.1 us (0.17); the launches traced: 525 us -> 90.7 us
  waiting for transfers between devices: 386 us -> 11.1 us
  matrix products: 46.5 us -> 0.93 us
  other arithmetic: 28.2 us -> 0.43 us
  blocking collectives: 24.8 us -> 46.4 us
  starting transfers between devices: 22.2 us -> 3.65 us
  Pallas kernels: 0 us -> 17.5 us
  between operations: 15.7 us -> 0.12 us
  local copies, waits for them, and re-layouts: 1.48 us -> 10.6 us
    reduce_scatter x3 -> x0, waiting for transfers between devices: 290 us -> none  [on_device(): lax.psum_scatter(project_lags(lag_table(lag_count * lax.axis_size('win'),...]
    psum x1 -> x0, waiting for transfers between devices: 91.2 us -> none  [from_root(): return lax.psum(block, axis)]
    dot_general x19 -> x1, matrix products: 46.5 us -> 0.93 us  [on_device(): jnp.einsum('tj,sbj->stb', basis, total, precision=lax.Precision.HIGHEST)]
    all_to_all x2, blocking collectives: 24.8 us -> 46.4 us  [the longest x1 27.9 us: on_device(): binned = lax.all_to_all(binned, ('win', 'chan'), 0, 0, tiled=True)]
    all_to_all x4 -> x1, starting transfers between devices: 21.5 us -> 3.65 us  [on_device(): total = lax.all_to_all(total, 'win', 0, 0, tiled=True)]
    pallas_call x0 -> x2, Pallas kernels: none -> 17.5 us  [the longest x1 13.3 us: bin_pairs(): pl.pallas_call(pairs_kernel, in_specs=[pl.BlockSpec(memory_space=pltpu.SM...]
    another operation x2 -> x0, other arithmetic: 10.2 us -> none
    cos x1 -> x0, other arithmetic: 9.38 us -> none  [lag_table(): jnp.cos(angles)]
  transfers between devices with their start and end apart: 8 -> 1, of which waited for: 6 -> 1; matrix products, arithmetic and copies ran while one was open for 9% -> 0% of each run, Pallas kernels for 0% -> 0%
where the time goes in v1:
time: 91.1 us; the launch traced here: 90.7 us
  blocking collectives  46.4 us (51%)
  Pallas kernels  17.5 us (19%)
  waiting for transfers between devices  11.1 us (12%)
  local copies, waits for them, and re-layouts  10.6 us (12%)
  starting transfers between devices  3.65 us (4%)
  matrix products  0.93 us (1%)
    all_to_all x1, blocking collectives, on_device(): binned = lax.all_to_all(binned, ('win', 'chan'), 0, 0, tiled=True)  27.9 us
    all_to_all x1, blocking collectives, on_device(): blocks = lax.all_to_all(blocks, 'chan', 0, 0, tiled=True)  18.5 us
    pallas_call x1, Pallas kernels, bin_pairs(): pl.pallas_call(pairs_kernel, in_specs=[pl.BlockSpec(memory_space=pltpu.SM...  13.3 us
    all_to_all x1, waiting for transfers between devices, on_device(): total = lax.all_to_all(total, 'win', 0, 0, tiled=True)  11.1 us
    unnamed x10, local copies, waits for them, and re-layouts  4.98 us
    pallas_call x1, Pallas kernels, whiten(): pl.pallas_call(whiten_kernel, grid=(WIN_DEV // 2,), in_specs=[pl.BlockSpe...  4.26 us
    all_to_all x1, starting transfers between devices, on_device(): total = lax.all_to_all(total, 'win', 0, 0, tiled=True)  3.65 us
  transfers between devices with their start and end apart: 1, of which 1 were waited for; matrix products, arithmetic and copies ran while one was open for 0% of the time, Pallas kernels for 0%

profile of v1, /device:TPU:1, one launch (start us, length us, event | category | flops | bytes accessed | tf_op | source)
XLA Modules:
  0.0 90.7 jit_solution(14721719925105326817)
XLA Ops:
  0.0 0.0 copy-start.2
  0.0 0.9 %copy.16.slot_ref = s32[1024,1]{1,0:T(8,128)S(1)} copy(s32[1024,1]{0,1:T(1,128)} %bitcast.25) | data formatting | bytes 8192 | tf_op jit(solution)/shard_map/reshape | solution.py:111
  0.9 0.7 reshape.40.source_ref
  1.6 0.7 reshape.41.receiver_ref
  2.3 0.7 reshape.42.bin_ref
  3.0 0.0 copy-start
  3.0 3.4 %copy-done = bf16[8,128,4096]{2,1,0:T(8,128)(2,1)S(1)} copy-done((bf16[8,128,4096]{2,1,0:T(8,128)(2,1)S(1)}, bf16[8,128,4096]{2,1,0:T(8,128)(2,1)}, u32[]{:S(2)}) %copy-start) | copy-done | bytes 8388632
  6.4 0.0 copy-start.1
  6.4 1.6 %copy-done.1 = bf16[256,4096]{1,0:T(8,128)(2,1)S(1)} copy-done((bf16[256,4096]{1,0:T(8,128)(2,1)S(1)}, bf16[256,4096]{1,0:T(8,128)(2,1)}, u32[]{:S(2)}) %copy-start.1) | copy-done | bytes 2097176
  8.0 0.0 copy-start.3
  8.0 0.0 copy-start.4
  8.0 4.3 %shard_map.91 = bf16[8,304,128]{2,1,0:T(8,128)(2,1)S(1)} custom-call(bf16[8,128,4096]{2,1,0:T(8,128)(2,1)S(1)} %copy-done, bf16[256,4096]{1,0:T(8,128)(2,1)S(1)} %copy-done.1, s32[1024,1]{1,0:T(8,128)S(1)} %copy.16.slot_ref, s32[3,1,512]{2,1,0:T(1,128)S(1)} %reshape.40.source_ref, s32[3,1,512]{2,1,0:T(1,128)S(1)} %reshape.41.receiver_ref, ...), custom_call_target="tpu_custom_call" | custom-call | tf_op jit(solution)/shard_map/pallas_call | solution.py:94
  12.3 18.5 %all_to_all.15.y_ref = bf16[8,304,128]{2,1,0:T(8,128)(2,1)S(1)} all-to-all(bf16[8,304,128]{2,1,0:T(8,128)(2,1)S(1)} %shard_map.91), channel_id=1, replica_groups=mesh['win'=32,'chan'=8] {'chan'}, dimensions={0} | all-to-all | bytes 1245184 | tf_op jit(solution)/shard_map/all_to_all | solution.py:178
  30.8 0.0 copy-done.2
  30.8 13.3 %shard_map.92 = bf16[256,384]{1,0:T(8,128)(2,1)S(1)} custom-call(s32[3]{0:T(128)S(1)} %copy-done.2, bf16[8,304,128]{2,1,0:T(8,128)(2,1)S(1)} %all_to_all.15.y_ref), custom_call_target="tpu_custom_call" | custom-call | tf_op jit(solution)/shard_map/pallas_call | solution.py:163
  44.1 0.1 copy.17
  44.2 0.2 copy.18
  44.4 27.9 %all_to_all.16 = bf16[256,3,128]{2,1,0:T(4,128)(2,1)S(1)} all-to-all(bf16[256,3,128]{2,1,0:T(4,128)(2,1)S(1)} %copy.18), channel_id=1, replica_groups=mesh['win'=32,'chan'=8] {'win','chan'}, dimensions={0} | all-to-all | bytes 393216 | tf_op jit(solution)/shard_map/all_to_all | solution.py:181
  72.3 0.3 convert_element_type.23
  72.6 0.4 reduce
  73.1 0.1 convert_element_type.27
  73.2 0.7 broadcast_in_dim.7
  73.9 3.7 %all-to-all-start.2 = ((bf16[32,12,256]{2,1,0:T(8,128)(2,1)}), bf16[32,12,256]{2,1,0:T(8,128)(2,1)S(1)}, u32[]{:S(2)}, u32[]{:S(2)}) async-start(bf16[32,12,256]{2,1,0:T(8,128)(2,1)} %broadcast_in_dim.7), calls=%async_computation.2 | async-start | bytes 524288 | tf_op jit(solution)/shard_map/all_to_all | solution.py:187
  77.6 11.1 %all-to-all-done.2 = bf16[32,12,256]{2,1,0:T(8,128)(2,1)S(1)} async-done(((bf16[32,12,256]{2,1,0:T(8,128)(2,1)}), bf16[32,12,256]{2,1,0:T(8,128)(2,1)S(1)}, u32[]{:S(2)}, u32[]{:S(2)}) %all-to-all-start.2) | async-done | bytes 196640 | tf_op jit(solution)/shard_map/all_to_all | solution.py:187
  88.6 0.1 copy.21
  88.7 0.2 copy.22
  88.9 0.1 reshape.45
  88.9 0.0 copy-done.3
  88.9 0.0 copy-done.4
  88.9 0.9 %convolution_bitcast_fusion = f32[3,128,128]{1,2,0:T(8,128)S(1)} fusion(bf16[3,128,256]{2,1,0:T(8,128)(2,1)S(1)} %reshape.45, s32[128]{0:T(128)S(1)} %add_add_fusion, s32[256]{0:T(256)S(1)} %copy-done.3, pred[256]{0:T(512)(128)(4,1)S(1)} %copy-done.4), kind=kOutput, calls=%fused_computation | convolution fusion | flops 151552000 | bytes 395008 | tf_op jit(solution)/shard_map/tj,sbj->stb/dot_general | solution.py:191
  89.9 0.8 copy.23
  (3 shorter events, 0.0 us)
Async XLA Ops:
  0.0 30.8 %copy-start.2 = (s32[3]{0:T(128)S(1)}, s32[3]{0:T(128)}, u32[]{:S(2)}) copy-start(s32[3]{0:T(128)} %block_ref.1) | copy-start | bytes 40
  3.0 3.4 %copy-start = (bf16[8,128,4096]{2,1,0:T(8,128)(2,1)S(1)}, bf16[8,128,4096]{2,1,0:T(8,128)(2,1)}, u32[]{:S(2)}) copy-start(bf16[8,128,4096]{2,1,0:T(8,128)(2,1)} %x_ref.1) | copy-start | bytes 25165828
  6.4 1.6 %copy-start.1 = (bf16[256,4096]{1,0:T(8,128)(2,1)S(1)}, bf16[256,4096]{1,0:T(8,128)(2,1)}, u32[]{:S(2)}) copy-start(bf16[256,4096]{1,0:T(8,128)(2,1)} %constant.37.clone.table_ref) | copy-start | bytes 6291460
  8.0 80.9 %copy-start.3 = (s32[256]{0:T(256)S(1)}, s32[256]{0:T(256)}, u32[]{:S(2)}) copy-start(s32[256]{0:T(256)} %constant.38.clone) | copy-start | bytes 3076
  8.0 80.9 %copy-start.4 = (pred[256]{0:T(512)(128)(4,1)S(1)}, pred[256]{0:T(512)(128)(4,1)}, u32[]{:S(2)}) copy-start(pred[256]{0:T(512)(128)(4,1)} %constant.39.clone) | copy-start | bytes 772
  73.9 14.7 %all-to-all-start.2 = ((bf16[32,12,256]{2,1,0:T(8,128)(2,1)}), bf16[32,12,256]{2,1,0:T(8,128)(2,1)S(1)}, u32[]{:S(2)}, u32[]{:S(2)}) async-start(bf16[32,12,256]{2,1,0:T(8,128)(2,1)} %broadcast_in_dim.7), calls=%async_computation.2 | async-start | bytes 524288 | tf_op jit(solution)/shard_map/all_to_all | solution.py:187

commit v2 on v0

v2 whole, which is shorter than its diff:
```python
import math

import jax
import jax.numpy as jnp
import numpy as np
from jax import lax
from jax.experimental import pallas as pl
from jax.experimental.pallas import tpu as pltpu
from jax.sharding import Mesh
from jax.sharding import PartitionSpec as P

WLEN = 4096
F = 128
FREQ0 = 256
LAGS = 4096
CH_DEV = 128
BIN_DEV = 128
STEPS = 3
WIN_DEV = 8
P_DEV = 512
BINS = 1024
N_WIN = 32
N_CHAN = 8
N_B = 8
N_A = N_WIN // N_B

GROUPS = N_A * N_CHAN
FG = F // GROUPS
COLS = 2 * FG
HALF = WIN_DEV * FG
ROWS = 2 * HALF
META = 16
QUARTERS = P_DEV // 128
SUB = BIN_DEV // N_B
TARGETS = N_B * N_CHAN
KCOLS = N_CHAN * COLS
PACKED = STEPS * SUB // 2
NT = (((1,), (1,)), ((), ()))
BF = jnp.bfloat16
F32 = jnp.float32
VMEM = pl.BlockSpec(memory_space=pltpu.VMEM)
SMEM = pl.BlockSpec(memory_space=pltpu.SMEM)
ANY = pl.BlockSpec(memory_space=pl.ANY)


def forward_rows():
    phases = (FREQ0 + np.arange(F))[:, None] * np.arange(WLEN)[None, :] % WLEN
    angles = phases.astype(np.float32) * np.float32(2.0 * math.pi / WLEN)
    return np.concatenate([np.cos(angles), -np.sin(angles)], axis=0).astype(BF)


def lag_tables():
    shape = (N_A, 2, N_CHAN, 2, FG)
    a, _, k, part, f = np.meshgrid(*[np.arange(n) for n in shape], indexing="ij")
    freq = (FREQ0 + FG * (a * N_CHAN + k) + f).reshape(-1)
    part = part.reshape(-1)
    block = LAGS // N_WIN
    inner = 2.0 * math.pi / WLEN * (freq[None, :] * np.arange(block)[:, None] % WLEN)
    starts = np.arange(N_WIN)[:, None] * block + (WLEN - LAGS // 2)
    outer = 2.0 * math.pi / WLEN * (freq[None, :] * starts % WLEN)
    norm_scale = 1.0 / math.sqrt(2.0 * F * N_WIN * WIN_DEV)
    first = np.where(part == 0, np.cos(outer), -np.sin(outer)) * norm_scale
    second = np.where(part == 0, -np.sin(outer), -np.cos(outer)) * norm_scale
    tables = np.cos(inner), np.sin(inner), first, second
    return [t.astype(np.float32) for t in tables]


def whiten_kernel(
    place_ref, x_hbm, table_hbm, slot_ref, source_ref, receiver_ref, bin_ref,
    out_ref, x_ref, table_ref, even_ref, x_sem, table_sem,
):
    table_copy = pltpu.make_async_copy(table_hbm, table_ref, table_sem)
    x_copies = [
        pltpu.make_async_copy(x_hbm.at[pl.ds(2 * i, 2)], x_ref.at[pl.ds(2 * i, 2)], x_sem.at[i])
        for i in range(WIN_DEV // 2)
    ]
    table_copy.start()
    for copy in x_copies:
        copy.start()

    slots = slot_ref[...]
    owner, low = slots // BIN_DEV, slots % BIN_DEV
    target = low // 8 % N_B * N_CHAN + owner
    sub = low // 64 * 8 + low % 8
    tables = jnp.concatenate([target, sub], axis=0).astype(F32).astype(BF)
    lane = lax.broadcasted_iota(jnp.int32, (128, P_DEV), 0)
    high = lax.broadcasted_iota(jnp.int32, (8, P_DEV), 0)
    place = place_ref[0]
    pieces = []
    for s in range(STEPS):
        bins = bin_ref[s : s + 1, :]
        onehot = jnp.where(lane == bins % 128, 1.0, 0.0).astype(BF)
        found = jnp.dot(tables, onehot, preferred_element_type=F32)
        here = high == bins // 128
        targets = jnp.sum(jnp.where(here, found[:8], 0.0), axis=0, keepdims=True)
        subs = jnp.sum(jnp.where(here, found[8:], 0.0), axis=0, keepdims=True)
        row = jnp.where(
            place < 2,
            jnp.where(place == 0, source_ref[s : s + 1, :], receiver_ref[s : s + 1, :]).astype(F32),
            jnp.where(place == 2, targets, subs),
        )
        pieces += [row[:, q * 128 : (q + 1) * 128] for q in range(QUARTERS)]
    pieces.append(jnp.zeros((META - len(pieces), 128), F32))
    block = jnp.concatenate(pieces, axis=0).astype(BF)
    for group in range(GROUPS):
        out_ref[group, ROWS:, :] = block

    table_copy.wait()
    upper = lax.broadcasted_iota(jnp.int32, (1, 8, 128), 1) < FG
    for i in range(WIN_DEV // 2):
        x_copies[i].wait()
        rows = x_ref[2 * i : 2 * i + 2].reshape(2 * CH_DEV, WLEN)
        spectra = lax.dot_general(table_ref[...], rows, NT, preferred_element_type=F32)
        power = jnp.sum(spectra * spectra, axis=0, keepdims=True) * (1.0 / (2 * F))
        whitened = (spectra * lax.rsqrt(power + 1e-06)).reshape(2 * F // 8, 8, 2 * CH_DEV)
        first, second = whitened[:, :, :CH_DEV], whitened[:, :, CH_DEV:]
        ours = [
            jnp.where(upper, first, jnp.roll(second, FG, axis=1)),
            jnp.where(upper, jnp.roll(first, FG, axis=1), second),
        ]
        for g in range(2):
            if i % 2 == 0:
                even_ref[g] = ours[g]
            else:
                both = jnp.concatenate([even_ref[g], ours[g]], axis=1).astype(BF)
                at = i // 2 * 16
                for pair in range(GROUPS // 2):
                    group = 2 * pair + g
                    out_ref[group, at : at + 16, :] = both[pair]
                    out_ref[group, HALF + at : HALF + at + 16, :] = both[GROUPS // 2 + pair]


def whiten(place, traces, pair_source, pair_receiver, pair_bin, bin_slot):
    return pl.pallas_call(
        whiten_kernel,
        in_specs=[SMEM, ANY, ANY, VMEM, VMEM, VMEM, VMEM],
        out_specs=VMEM,
        out_shape=jax.ShapeDtypeStruct((GROUPS, ROWS + META, CH_DEV), BF),
        scratch_shapes=[
            pltpu.VMEM((WIN_DEV, CH_DEV, WLEN), BF),
            pltpu.VMEM((2 * F, WLEN), BF),
            pltpu.VMEM((2, 2 * F // 8, 8, CH_DEV), F32),
            pltpu.SemaphoreType.DMA((WIN_DEV // 2,)),
            pltpu.SemaphoreType.DMA(()),
        ],
        compiler_params=pltpu.CompilerParams(vmem_limit_bytes=56 << 20),
    )(
        place, traces, jnp.asarray(forward_rows()), bin_slot.reshape(8, 128),
        pair_source, pair_receiver, pair_bin,
    )


def pairs_kernel(block_ref, y_ref, out_ref, source_ref):
    index = lax.broadcasted_iota(jnp.int32, (128, 128), 0).astype(F32).astype(BF)
    low_half = lax.broadcasted_iota(jnp.int32, (8, P_DEV), 0) < FG
    lower_row = (lax.broadcasted_iota(jnp.int32, (16, 128), 0) // 8).astype(F32)
    one, zero = jnp.ones((), BF), jnp.zeros((), BF)

    def spread(row, count):
        columns = []
        for q in range(QUARTERS):
            entry = jnp.broadcast_to(row[q : q + 1], (16, 128)).astype(BF)
            entry = jnp.concatenate([entry] * (count // 16), axis=0)
            columns.append(jnp.where(index[:count] == entry, one, zero))
        return jnp.concatenate(columns, axis=1)

    for s in range(STEPS):
        block = block_ref[s]
        for a in range(N_A):
            source_ref[a * ROWS : (a + 1) * ROWS, :] = y_ref[a, block, :ROWS, :]

        def body(c, total):
            lists = [
                y_ref[kind, c, ROWS:, :].astype(F32)[s * QUARTERS : (s + 1) * QUARTERS]
                for kind in range(4)
            ]
            receiver = jnp.concatenate([y_ref[a, c, :ROWS, :] for a in range(N_A)], axis=0)
            u = jnp.dot(source_ref[...], spread(lists[0], CH_DEV), preferred_element_type=F32)
            v = jnp.dot(receiver, spread(lists[1], CH_DEV), preferred_element_type=F32)
            real_part = jnp.zeros((8, P_DEV), F32)
            imag_part = jnp.zeros((8, P_DEV), F32)
            for a in range(N_A):
                for r in range(0, HALF, 8):
                    at = a * ROWS + r
                    u_re, u_im = u[at : at + 8], u[at + HALF : at + HALF + 8]
                    v_re, v_im = v[at : at + 8], v[at + HALF : at + HALF + 8]
                    real_part += u_re * v_re + u_im * v_im
                    imag_part += u_re * v_im - u_im * v_re
            real_part += jnp.roll(real_part, FG, axis=0)
            imag_part += jnp.roll(imag_part, FG, axis=0)
            partial = jnp.where(low_half, real_part, imag_part)
            partial = jnp.concatenate([partial, partial], axis=0).astype(BF)
            placed = []
            for q in range(QUARTERS):
                sub = (jnp.broadcast_to(lists[3][q : q + 1], (16, 128)) - lower_row).astype(BF)
                values = partial[:, q * 128 : (q + 1) * 128]
                placed.append(
                    jnp.concatenate(
                        [
                            jnp.where(sub == jnp.full((16, 128), float(k), BF), values, zero)
                            for k in range(0, SUB, 2)
                        ],
                        axis=0,
                    )
                )
            placed = jnp.concatenate(placed, axis=1)
            return total + lax.dot_general(
                spread(lists[2], TARGETS), placed, NT, preferred_element_type=F32
            )

        total = lax.fori_loop(
            0, N_CHAN, body, jnp.zeros((TARGETS, SUB * COLS), F32), unroll=2
        )
        out_ref[:, s * 128 : (s + 1) * 128] = total.astype(BF)


def bin_pairs(source_block, chunks):
    return pl.pallas_call(
        pairs_kernel,
        in_specs=[SMEM, VMEM],
        out_specs=VMEM,
        out_shape=jax.ShapeDtypeStruct((TARGETS, STEPS * SUB * COLS), BF),
        scratch_shapes=[pltpu.VMEM((N_A * ROWS, CH_DEV), BF)],
        compiler_params=pltpu.CompilerParams(vmem_limit_bytes=32 << 20),
    )(source_block, chunks)


def sum_kernel(part_ref, out_ref):
    parts = part_ref[...].astype(F32).reshape(N_B, N_CHAN, STEPS * 128)
    total = jnp.sum(parts, axis=0).astype(BF).astype(F32)
    lane = lax.broadcasted_iota(jnp.int32, (SUB, 128), 1)
    here = lane // COLS == lax.broadcasted_iota(jnp.int32, (SUB, 128), 0)
    wide = []
    for k in range(N_CHAN):
        rows = [
            jnp.where(here, total[k : k + 1, s * 128 : (s + 1) * 128], 0.0) for s in range(STEPS)
        ]
        wide.append(jnp.concatenate(rows, axis=0).astype(BF))
    wide = jnp.concatenate(wide, axis=1)
    row = lax.broadcasted_iota(jnp.int32, (N_CHAN * 128, KCOLS), 0)
    column = lax.broadcasted_iota(jnp.int32, (N_CHAN * 128, KCOLS), 1)
    fold = (row % COLS == column % COLS) & (row // 128 == column // COLS)
    fold = jnp.where(fold, 1.0, 0.0).astype(BF)
    packed = jnp.dot(wide, fold, preferred_element_type=F32)
    packed = jnp.concatenate([packed[:PACKED], packed[PACKED:]], axis=1).astype(BF)
    for w in range(N_WIN):
        out_ref[w] = packed


def sum_windows(parts):
    return pl.pallas_call(
        sum_kernel,
        in_specs=[VMEM],
        out_specs=VMEM,
        out_shape=jax.ShapeDtypeStruct((N_WIN, PACKED, 128), BF),
    )(parts)


def lag_kernel(place_ref, bins_ref, cos_ref, sin_ref, first_ref, second_ref, out_ref):
    place = place_ref[0]
    basis = (
        cos_ref[...] * first_ref[pl.ds(place, 1), :]
        + sin_ref[...] * second_ref[pl.ds(place, 1), :]
    )
    upper = basis.astype(BF)
    rest = (basis - upper.astype(F32)).astype(BF)
    lane_half = lax.broadcasted_iota(jnp.int32, (64, 128), 1) // KCOLS
    for s in range(STEPS):
        pieces = []
        for part in range(2):
            first = s * SUB + part * 8
            half, at = first // PACKED, first % PACKED
            columns = []
            for a in range(N_A):
                rows = [
                    bins_ref[b * N_A + a].astype(F32)[at : at + 8] for b in range(N_B)
                ]
                rows = jnp.concatenate(rows, axis=0)
                columns.append(jnp.where(lane_half == half, rows, 0.0).astype(BF))
            pieces.append(jnp.concatenate(columns, axis=1))
        binned = jnp.concatenate(pieces, axis=0)
        out_ref[s] = lax.dot_general(
            upper, binned, NT, preferred_element_type=F32
        ) + lax.dot_general(rest, binned, NT, preferred_element_type=F32)


def project_lags(place, bins):
    return pl.pallas_call(
        lag_kernel,
        in_specs=[SMEM] + [VMEM] * 5,
        out_specs=VMEM,
        out_shape=jax.ShapeDtypeStruct((STEPS, LAGS // N_WIN, BIN_DEV), F32),
        compiler_params=pltpu.CompilerParams(vmem_limit_bytes=32 << 20),
    )(place, bins, *[jnp.asarray(t) for t in lag_tables()])


def on_device(traces, source_block, pair_source, pair_receiver, pair_bin, bin_slot):
    place_a = lax.axis_index("a").reshape(1)
    place_win = lax.axis_index(("b", "a")).reshape(1)
    chunks = whiten(place_a, traces, pair_source, pair_receiver, pair_bin, bin_slot)
    chunks = lax.all_to_all(chunks, ("a", "chan"), 0, 0, tiled=True)
    parts = bin_pairs(source_block, chunks.reshape(N_A, N_CHAN, ROWS + META, CH_DEV))
    parts = lax.all_to_all(
        parts.reshape(TARGETS, STEPS, 128), ("b", "chan"), 0, 0, tiled=True
    )
    bins = sum_windows(parts.reshape(TARGETS, STEPS * 128))
    bins = lax.all_to_all(bins, ("b", "a"), 0, 0, tiled=True)
    return project_lags(place_win, bins)


def solution(mesh):
    split = Mesh(mesh.devices.reshape(N_B, N_A, N_CHAN), ("b", "a", "chan"))
    win = ("b", "a")
    placed = (P(win, "chan", None), P(), P(None, "chan"), P(None, "chan"), P(None, "chan"), P())
    return jax.shard_map(
        on_device, mesh=split, in_specs=placed, out_specs=P(None, win, "chan"), check_vma=False
    )
```

time: 536 us -> 83.5 us (0.16); the launches traced: 525 us -> 83.1 us
  waiting for transfers between devices: 386 us -> 10.4 us
  matrix products: 46.5 us -> 0 us
  other arithmetic: 28.2 us -> 0 us
  Pallas kernels: 0 us -> 23.6 us
  blocking collectives: 24.8 us -> 42.8 us
  starting transfers between devices: 22.2 us -> 5.62 us
  between operations: 15.7 us -> 0.08 us
    reduce_scatter x3 -> x0, waiting for transfers between devices: 290 us -> none  [on_device(): lax.psum_scatter(project_lags(lag_table(lag_count * lax.axis_size('win'),...]
    psum x1 -> x0, waiting for transfers between devices: 91.2 us -> none  [from_root(): return lax.psum(block, axis)]
    dot_general x19 -> x0, matrix products: 46.5 us -> none  [the longest x3 28.9 us: project_lags(): lax.dot_general(lag_basis, binned, (((0,), (1,)), ((), ())), precision=la...]
    pallas_call x0 -> x4, Pallas kernels: none -> 23.6 us  [the longest x1 10.4 us: whiten(): pl.pallas_call(whiten_kernel, in_specs=[SMEM, ANY, ANY, VMEM, VMEM, VMEM,...]
    all_to_all x2, blocking collectives: 24.8 us -> 42.8 us  [the longest x1 22 us: on_device(): chunks = lax.all_to_all(chunks, ('a', 'chan'), 0, 0, tiled=True)]
    all_to_all x4 -> x1, starting transfers between devices: 21.5 us -> 5.62 us  [on_device(): bins = lax.all_to_all(bins, ('b', 'a'), 0, 0, tiled=True)]
    another operation x2 -> x0, other arithmetic: 10.2 us -> none
    cos x1 -> x0, other arithmetic: 9.38 us -> none  [lag_table(): jnp.cos(angles)]
  transfers between devices with their start and end apart: 8 -> 1, of which waited for: 6 -> 1; matrix products, arithmetic and copies ran while one was open for 9% -> 0% of each run, Pallas kernels for 0% -> 0%
where the time goes in v2:
time: 83.5 us; the launch traced here: 83.1 us
  blocking collectives  42.8 us (51%)
  Pallas kernels  23.6 us (28%)
  waiting for transfers between devices  10.4 us (12%)
  starting transfers between devices  5.62 us (7%)
    all_to_all x1, blocking collectives, on_device(): chunks = lax.all_to_all(chunks, ('a', 'chan'), 0, 0, tiled=True)  22 us
    all_to_all x1, blocking collectives, on_device(): lax.all_to_all(parts.reshape(TARGETS, STEPS, 128), ('b', 'chan'), 0, 0, t...  20.8 us
    pallas_call x1, Pallas kernels, whiten(): pl.pallas_call(whiten_kernel, in_specs=[SMEM, ANY, ANY, VMEM, VMEM, VMEM,...  10.4 us
    all_to_all x1, waiting for transfers between devices, on_device(): bins = lax.all_to_all(bins, ('b', 'a'), 0, 0, tiled=True)  10.4 us
    pallas_call x1, Pallas kernels, bin_pairs(): pl.pallas_call(pairs_kernel, in_specs=[SMEM, VMEM], out_specs=VMEM, out_s...  10.3 us
    all_to_all x1, starting transfers between devices, on_device(): bins = lax.all_to_all(bins, ('b', 'a'), 0, 0, tiled=True)  5.62 us
    pallas_call x1, Pallas kernels, sum_windows(): pl.pallas_call(sum_kernel, in_specs=[VMEM], out_specs=VMEM, out_shape=jax...  1.81 us
  transfers between devices with their start and end apart: 1, of which 1 were waited for; matrix products, arithmetic and copies ran while one was open for 0% of the time, Pallas kernels for 0%

profile of v2, /device:TPU:1, one launch (start us, length us, event | category | flops | bytes accessed | tf_op | source)
XLA Modules:
  0.0 83.1 jit_solution(12150320291832174325)
XLA Ops:
  0.0 0.0 copy-start.2
  0.0 0.0 copy-start.3
  0.0 0.0 copy-start
  0.0 0.0 copy-start.1
  0.0 0.0 copy-start.4
  0.0 10.4 %shard_map.109 = bf16[32,80,128]{2,1,0:T(8,128)(2,1)} custom-call(s32[1]{0:T(128)} %bitcast.1.place_ref, bf16[8,128,4096]{2,1,0:T(8,128)(2,1)} %x_hbm.1, bf16[256,4096]{1,0:T(8,128)(2,1)} %constant.22.clone.table_hbm, s32[8,128]{1,0:T(8,128)} %bitcast.11, s32[3,512]{1,0:T(4,128)} %source_ref.1, s32[3,512]{1,0:T(4,128)} %receiver_ref.1, s32[3,512]{1,0:T(4,128)} %bin_ref.1), custom_call_target="tpu_custom_call" | custom-call | tf_op jit(solution)/shard_map/pallas_call | solution.py:134
  10.5 22.0 %all_to_all.15 = bf16[32,80,128]{2,1,0:T(8,128)(2,1)S(1)} all-to-all(bf16[32,80,128]{2,1,0:T(8,128)(2,1)} %shard_map.109), channel_id=1, replica_groups=mesh['b'=8,'a'=4,'chan'=8] {'a','chan'}, dimensions={0} | all-to-all | bytes 1310720 | tf_op jit(solution)/shard_map/all_to_all | solution.py:301
  32.4 0.0 copy-done.4
  32.4 10.3 %shard_map.110 = bf16[64,384]{1,0:T(8,128)(2,1)S(1)} custom-call(s32[3]{0:T(128)S(1)} %copy-done.4, bf16[4,8,80,128]{3,2,1,0:T(8,128)(2,1)S(1)} %bitcast.8), custom_call_target="tpu_custom_call" | custom-call | tf_op jit(solution)/shard_map/pallas_call | solution.py:218
  42.8 20.8 %all_to_all.16 = bf16[64,3,128]{2,1,0:T(4,128)(2,1)S(1)} all-to-all(bf16[64,3,128]{2,1,0:T(4,128)(2,1)S(1)} %reshape.22), channel_id=1, replica_groups=mesh['b'=8,'a'=4,'chan'=8] {'b','chan'}, dimensions={0} | all-to-all | bytes 98304 | tf_op jit(solution)/shard_map/all_to_all | solution.py:303
  63.6 0.6 copy.14
  64.2 1.8 %shard_map.111 = bf16[32,24,128]{2,1,0:T(8,128)(2,1)} custom-call(bf16[64,384]{1,0:T(8,128)(2,1)} %bitcast.10), custom_call_target="tpu_custom_call" | custom-call | tf_op jit(solution)/shard_map/pallas_call | solution.py:251
  66.0 5.6 %all-to-all-start.2 = ((bf16[32,24,128]{2,1,0:T(8,128)(2,1)}), bf16[32,24,128]{2,1,0:T(8,128)(2,1)S(1)}, u32[]{:S(2)}, u32[]{:S(2)}) async-start(bf16[32,24,128]{2,1,0:T(8,128)(2,1)} %shard_map.111), calls=%async_computation.2 | async-start | bytes 393216 | tf_op jit(solution)/shard_map/all_to_all | solution.py:307
  71.7 10.4 %all-to-all-done.2.bins_ref = bf16[32,24,128]{2,1,0:T(8,128)(2,1)S(1)} async-done(((bf16[32,24,128]{2,1,0:T(8,128)(2,1)}), bf16[32,24,128]{2,1,0:T(8,128)(2,1)S(1)}, u32[]{:S(2)}, u32[]{:S(2)}) %all-to-all-start.2) | async-done | bytes 196640 | tf_op jit(solution)/shard_map/all_to_all | solution.py:307
  82.0 0.0 copy-done.2
  82.0 0.0 copy-done.3
  82.0 0.0 copy-done
  82.0 0.0 copy-done.1
  82.1 1.0 %shard_map.112 = f32[3,128,128]{2,1,0:T(8,128)} custom-call(s32[1]{0:T(128)} %bitcast.place_ref, bf16[32,24,128]{2,1,0:T(8,128)(2,1)S(1)} %all-to-all-done.2.bins_ref, f32[128,512]{1,0:T(8,128)S(1)} %copy-done.1, f32[128,512]{1,0:T(8,128)S(1)} %copy-done, f32[32,512]{1,0:T(8,128)S(1)} %copy-done.3, f32[32,512]{1,0:T(8,128)S(1)} %copy-done.2), custom_call_target="tpu_custom_call" | custom-call | tf_op jit(solution)/shard_map/pallas_call | solution.py:288
  (1 shorter events, 0.0 us)
Async XLA Ops:
  0.0 82.0 %copy-start.2 = (f32[32,512]{1,0:T(8,128)S(1)}, f32[32,512]{1,0:T(8,128)}, u32[]{:S(2)}) copy-start(f32[32,512]{1,0:T(8,128)} %constant.26.clone.second_ref) | copy-start | bytes 196612
  0.0 82.0 %copy-start.3 = (f32[32,512]{1,0:T(8,128)S(1)}, f32[32,512]{1,0:T(8,128)}, u32[]{:S(2)}) copy-start(f32[32,512]{1,0:T(8,128)} %constant.25.clone.first_ref) | copy-start | bytes 196612
  0.0 82.0 %copy-start = (f32[128,512]{1,0:T(8,128)S(1)}, f32[128,512]{1,0:T(8,128)}, u32[]{:S(2)}) copy-start(f32[128,512]{1,0:T(8,128)} %constant.24.clone.sin_ref) | copy-start | bytes 786436
  0.0 82.0 %copy-start.1 = (f32[128,512]{1,0:T(8,128)S(1)}, f32[128,512]{1,0:T(8,128)}, u32[]{:S(2)}) copy-start(f32[128,512]{1,0:T(8,128)} %constant.23.clone.cos_ref) | copy-start | bytes 786436
  0.0 32.4 %copy-start.4 = (s32[3]{0:T(128)S(1)}, s32[3]{0:T(128)}, u32[]{:S(2)}) copy-start(s32[3]{0:T(128)} %block_ref.1) | copy-start | bytes 40
  66.0 16.0 %all-to-all-start.2 = ((bf16[32,24,128]{2,1,0:T(8,128)(2,1)}), bf16[32,24,128]{2,1,0:T(8,128)(2,1)S(1)}, u32[]{:S(2)}, u32[]{:S(2)}) async-start(bf16[32,24,128]{2,1,0:T(8,128)(2,1)} %shard_map.111), calls=%async_computation.2 | async-start | bytes 393216 | tf_op jit(solution)/shard_map/all_to_all | solution.py:307

commit v3 on v2

--- a/solution.py
+++ b/solution.py
@@ -40,13 +40,16 @@
 F32 = jnp.float32
 VMEM = pl.BlockSpec(memory_space=pltpu.VMEM)
 SMEM = pl.BlockSpec(memory_space=pltpu.SMEM)
-ANY = pl.BlockSpec(memory_space=pl.ANY)
-
-
-def forward_rows():
-    phases = (FREQ0 + np.arange(F))[:, None] * np.arange(WLEN)[None, :] % WLEN
-    angles = phases.astype(np.float32) * np.float32(2.0 * math.pi / WLEN)
-    return np.concatenate([np.cos(angles), -np.sin(angles)], axis=0).astype(BF)
+HBM = pl.BlockSpec(memory_space=pltpu.HBM)
+
+
+def forward_tables():
+    freq = (FREQ0 + np.arange(F))[:, None]
+    inner = 2.0 * math.pi / WLEN * (freq * np.arange(128)[None, :] % WLEN)
+    outer = 2.0 * math.pi / WLEN * (freq * np.arange(0, WLEN, 128)[None, :] % WLEN)
+    pad = np.zeros((F, 128 - 2 * outer.shape[1]))
+    tables = np.cos(inner), np.sin(inner), np.cos(outer), np.sin(outer), pad
+    return np.concatenate(tables, axis=1).astype(np.float32)
 
 
 def lag_tables():
@@ -66,17 +69,25 @@
 
 
 def whiten_kernel(
-    place_ref, x_hbm, table_hbm, slot_ref, source_ref, receiver_ref, bin_ref,
-    out_ref, x_ref, table_ref, even_ref, x_sem, table_sem,
+    place_ref, x_hbm, basis_hbm, slot_hbm, source_hbm, receiver_hbm, bin_hbm,
+    out_ref, x_ref, basis_ref, slot_ref, source_ref, receiver_ref, bin_ref,
+    table_ref, even_ref, x_sem, small_sem,
 ):
-    table_copy = pltpu.make_async_copy(table_hbm, table_ref, table_sem)
+    small = [
+        pltpu.make_async_copy(slot_hbm, slot_ref, small_sem.at[0]),
+        pltpu.make_async_copy(source_hbm, source_ref, small_sem.at[1]),
+        pltpu.make_async_copy(receiver_hbm, receiver_ref, small_sem.at[2]),
+        pltpu.make_async_copy(bin_hbm, bin_ref, small_sem.at[3]),
+        pltpu.make_async_copy(basis_hbm, basis_ref, small_sem.at[4]),
+    ]
     x_copies = [
         pltpu.make_async_copy(x_hbm.at[pl.ds(2 * i, 2)], x_ref.at[pl.ds(2 * i, 2)], x_sem.at[i])
         for i in range(WIN_DEV // 2)
     ]
-    table_copy.start()
-    for copy in x_copies:
+    for copy in small + x_copies[:2]:
         copy.start()
+    for copy in small:
+        copy.wait()
 
     slots = slot_ref[...]
     owner, low = slots // BIN_DEV, slots % BIN_DEV
@@ -105,10 +116,21 @@
     for group in range(GROUPS):
         out_ref[group, ROWS:, :] = block
 
-    table_copy.wait()
+    for copy in x_copies[2:]:
+        copy.start()
+    cos_in, sin_in = basis_ref[:, :128], basis_ref[:, 128:256]
+    starts = WLEN // 128
+    for q in range(starts):
+        cos_out = jnp.broadcast_to(basis_ref[:, 256 + q : 257 + q], (F, 128))
+        sin_out = jnp.broadcast_to(basis_ref[:, 256 + starts + q : 257 + starts + q], (F, 128))
+        lanes = slice(q * 128, (q + 1) * 128)
+        table_ref[:F, lanes] = (cos_out * cos_in - sin_out * sin_in).astype(BF)
+        table_ref[F:, lanes] = (-(sin_out * cos_in) - cos_out * sin_in).astype(BF)
     upper = lax.broadcasted_iota(jnp.int32, (1, 8, 128), 1) < FG
     for i in range(WIN_DEV // 2):
-        x_copies[i].wait()
+        if i % 2 == 0:
+            x_copies[i].wait()
+            x_copies[i + 1].wait()
         rows = x_ref[2 * i : 2 * i + 2].reshape(2 * CH_DEV, WLEN)
         spectra = lax.dot_general(table_ref[...], rows, NT, preferred_element_type=F32)
         power = jnp.sum(spectra * spectra, axis=0, keepdims=True) * (1.0 / (2 * F))
@@ -133,24 +155,35 @@
 def whiten(place, traces, pair_source, pair_receiver, pair_bin, bin_slot):
     return pl.pallas_call(
         whiten_kernel,
-        in_specs=[SMEM, ANY, ANY, VMEM, VMEM, VMEM, VMEM],
+        in_specs=[SMEM] + [HBM] * 6,
         out_specs=VMEM,
         out_shape=jax.ShapeDtypeStruct((GROUPS, ROWS + META, CH_DEV), BF),
         scratch_shapes=[
             pltpu.VMEM((WIN_DEV, CH_DEV, WLEN), BF),
+            pltpu.VMEM((F, 384), F32),
+            pltpu.VMEM((8, 128), jnp.int32),
+            pltpu.VMEM((STEPS, P_DEV), jnp.int32),
+            pltpu.VMEM((STEPS, P_DEV), jnp.int32),
+            pltpu.VMEM((STEPS, P_DEV), jnp.int32),
             pltpu.VMEM((2 * F, WLEN), BF),
             pltpu.VMEM((2, 2 * F // 8, 8, CH_DEV), F32),
             pltpu.SemaphoreType.DMA((WIN_DEV // 2,)),
-            pltpu.SemaphoreType.DMA(()),
+            pltpu.SemaphoreType.DMA((5,)),
         ],
-        compiler_params=pltpu.CompilerParams(vmem_limit_bytes=56 << 20),
+        compiler_params=pltpu.CompilerParams(vmem_limit_bytes=24 << 20),
     )(
-        place, traces, jnp.asarray(forward_rows()), bin_slot.reshape(8, 128),
-        pair_source, pair_receiver, pair_bin,
+        place,
+        *[
+            pltpu.with_memory_space_constraint(array, pltpu.HBM)
+            for array in (
+                traces, jnp.asarray(forward_tables()), bin_slot.reshape(8, 128),
+                pair_source, pair_receiver, pair_bin,
+            )
+        ],
     )
 
 
-def pairs_kernel(block_ref, y_ref, out_ref, source_ref):
+def pairs_kernel(block_ref, y_ref, out_ref, source_ref, placed_ref, target_ref):
     index = lax.broadcasted_iota(jnp.int32, (128, 128), 0).astype(F32).astype(BF)
     low_half = lax.broadcasted_iota(jnp.int32, (8, P_DEV), 0) < FG
     lower_row = (lax.broadcasted_iota(jnp.int32, (16, 128), 0) // 8).astype(F32)
@@ -169,7 +202,7 @@
         for a in range(N_A):
             source_ref[a * ROWS : (a + 1) * ROWS, :] = y_ref[a, block, :ROWS, :]
 
-        def body(c, total):
+        def body(c, carry):
             lists = [
                 y_ref[kind, c, ROWS:, :].astype(F32)[s * QUARTERS : (s + 1) * QUARTERS]
                 for kind in range(4)
@@ -186,32 +219,27 @@
                     v_re, v_im = v[at : at + 8], v[at + HALF : at + HALF + 8]
                     real_part += u_re * v_re + u_im * v_im
                     imag_part += u_re * v_im - u_im * v_re
-            real_part += jnp.roll(real_part, FG, axis=0)
-            imag_part += jnp.roll(imag_part, FG, axis=0)
+            real_part += pltpu.roll(real_part, FG, axis=0)
+            imag_part += pltpu.roll(imag_part, FG, axis=0)
             partial = jnp.where(low_half, real_part, imag_part)
             partial = jnp.concatenate([partial, partial], axis=0).astype(BF)
-            placed = []
             for q in range(QUARTERS):
                 sub = (jnp.broadcast_to(lists[3][q : q + 1], (16, 128)) - lower_row).astype(BF)
                 values = partial[:, q * 128 : (q + 1) * 128]
-                placed.append(
-                    jnp.concatenate(
-                        [
-                            jnp.where(sub == jnp.full((16, 128), float(k), BF), values, zero)
-                            for k in range(0, SUB, 2)
-                        ],
-                        axis=0,
+                lanes = pl.ds(pl.multiple_of(c * P_DEV + q * 128, 128), 128)
+                for k in range(0, SUB, 2):
+                    placed_ref[k * 8 : k * 8 + 16, lanes] = jnp.where(
+                        sub == jnp.full((16, 128), float(k), BF), values, zero
                     )
-                )
-            placed = jnp.concatenate(placed, axis=1)
-            return total + lax.dot_general(
-                spread(lists[2], TARGETS), placed, NT, preferred_element_type=F32
+            target_ref[:, pl.ds(pl.multiple_of(c * P_DEV, 128), P_DEV)] = spread(
+                lists[2], TARGETS
             )
-
-        total = lax.fori_loop(
-            0, N_CHAN, body, jnp.zeros((TARGETS, SUB * COLS), F32), unroll=2
-        )
-        out_ref[:, s * 128 : (s + 1) * 128] = total.astype(BF)
+            return carry
+
+        lax.fori_loop(0, N_CHAN, body, 0, unroll=8)
+        out_ref[:, s * 128 : (s + 1) * 128] = lax.dot_general(
+            target_ref[...], placed_ref[...], NT, preferred_element_type=F32
+        ).astype(BF)
 
 
 def bin_pairs(source_block, chunks):
@@ -220,20 +248,24 @@
         in_specs=[SMEM, VMEM],
         out_specs=VMEM,
         out_shape=jax.ShapeDtypeStruct((TARGETS, STEPS * SUB * COLS), BF),
-        scratch_shapes=[pltpu.VMEM((N_A * ROWS, CH_DEV), BF)],
+        scratch_shapes=[
+            pltpu.VMEM((N_A * ROWS, CH_DEV), BF),
+            pltpu.VMEM((SUB * COLS, N_CHAN * P_DEV), BF),
+            pltpu.VMEM((TARGETS, N_CHAN * P_DEV), BF),
+        ],
         compiler_params=pltpu.CompilerParams(vmem_limit_bytes=32 << 20),
     )(source_block, chunks)
 
 
 def sum_kernel(part_ref, out_ref):
-    parts = part_ref[...].astype(F32).reshape(N_B, N_CHAN, STEPS * 128)
+    parts = part_ref[...].astype(F32).reshape(N_B, N_CHAN, STEPS, 128)
     total = jnp.sum(parts, axis=0).astype(BF).astype(F32)
     lane = lax.broadcasted_iota(jnp.int32, (SUB, 128), 1)
     here = lane // COLS == lax.broadcasted_iota(jnp.int32, (SUB, 128), 0)
     wide = []
     for k in range(N_CHAN):
         rows = [
-            jnp.where(here, total[k : k + 1, s * 128 : (s + 1) * 128], 0.0) for s in range(STEPS)
+            jnp.where(here, total[k, s : s + 1], 0.0) for s in range(STEPS)
         ]
         wide.append(jnp.concatenate(rows, axis=0).astype(BF))
     wide = jnp.concatenate(wide, axis=1)
@@ -253,6 +285,7 @@
         in_specs=[VMEM],
         out_specs=VMEM,
         out_shape=jax.ShapeDtypeStruct((N_WIN, PACKED, 128), BF),
+        compiler_params=pltpu.CompilerParams(vmem_limit_bytes=8 << 20),
     )(parts)
 
 
@@ -303,7 +336,7 @@
     parts = lax.all_to_all(
         parts.reshape(TARGETS, STEPS, 128), ("b", "chan"), 0, 0, tiled=True
     )
-    bins = sum_windows(parts.reshape(TARGETS, STEPS * 128))
+    bins = sum_windows(parts)
     bins = lax.all_to_all(bins, ("b", "a"), 0, 0, tiled=True)
     return project_lags(place_win, bins)
 

time: 83.5 us -> 72.1 us (0.86)
  Pallas kernels: 23.6 us -> 13.2 us
    pallas_call x1, Pallas kernels: 10.3 us -> 5.28 us  [bin_pairs(): pl.pallas_call(pairs_kernel, in_specs=[SMEM, VMEM], out_specs=VMEM, out_s...]
    pallas_call x1, Pallas kernels: 10.4 us -> 5.81 us  [whiten(): pl.pallas_call(whiten_kernel, in_specs=[SMEM] + [HBM] * 6, out_specs=VMEM...]
where the time goes in v3:
time: 72.1 us; the launch traced here: 71.8 us
  blocking collectives  42.5 us (59%)
  Pallas kernels  13.2 us (18%)
  waiting for transfers between devices  10.4 us (14%)
  starting transfers between devices  5.64 us (8%)
    all_to_all x1, blocking collectives, on_device(): chunks = lax.all_to_all(chunks, ('a', 'chan'), 0, 0, tiled=True)  21.7 us
    all_to_all x1, blocking collectives, on_device(): lax.all_to_all(parts.reshape(TARGETS, STEPS, 128), ('b', 'chan'), 0, 0, t...  20.8 us
    all_to_all x1, waiting for transfers between devices, on_device(): bins = lax.all_to_all(bins, ('b', 'a'), 0, 0, tiled=True)  10.4 us
    pallas_call x1, Pallas kernels, whiten(): pl.pallas_call(whiten_kernel, in_specs=[SMEM] + [HBM] * 6, out_specs=VMEM...  5.81 us
    all_to_all x1, starting transfers between devices, on_device(): bins = lax.all_to_all(bins, ('b', 'a'), 0, 0, tiled=True)  5.64 us
    pallas_call x1, Pallas kernels, bin_pairs(): pl.pallas_call(pairs_kernel, in_specs=[SMEM, VMEM], out_specs=VMEM, out_s...  5.28 us
  transfers between devices with their start and end apart: 1, of which 1 were waited for; matrix products, arithmetic and copies ran while one was open for 0% of the time, Pallas kernels for 0%

profile of v3, /device:TPU:1, one launch (start us, length us, event | category | flops | bytes accessed | tf_op | source)
XLA Modules:
  0.0 71.8 jit_solution(13015406383651286151)
XLA Ops:
  0.0 0.0 copy-start.2
  0.0 0.0 copy-start.3
  0.0 0.0 copy-start
  0.0 0.0 copy-start.1
  0.0 0.0 copy-start.4
  0.0 5.8 %shard_map.109 = bf16[32,80,128]{2,1,0:T(8,128)(2,1)S(1)} custom-call(s32[1]{0:T(128)} %bitcast.1.place_ref, bf16[8,128,4096]{2,1,0:T(8,128)(2,1)} %x_hbm.1, f32[128,384]{1,0:T(8,128)} %constant.22.clone.basis_hbm, s32[8,128]{1,0:T(8,128)} %bitcast.5, s32[3,512]{1,0:T(4,128)} %source_hbm.1, s32[3,512]{1,0:T(4,128)} %receiver_hbm.1, s32[3,512]{1,0:T(4,128)} %bin_hbm.1), custom_call_target="tpu_custom_call" | custom-call | tf_op jit(solution)/shard_map/pallas_call | solution.py:156
  5.9 21.7 %all_to_all.15 = bf16[32,80,128]{2,1,0:T(8,128)(2,1)S(1)} all-to-all(bf16[32,80,128]{2,1,0:T(8,128)(2,1)S(1)} %shard_map.109), channel_id=1, replica_groups=mesh['b'=8,'a'=4,'chan'=8] {'a','chan'}, dimensions={0} | all-to-all | bytes 1310720 | tf_op jit(solution)/shard_map/all_to_all | solution.py:334
  27.6 0.0 copy-done.4
  27.6 5.3 %shard_map.110 = bf16[64,384]{1,0:T(8,128)(2,1)S(1)} custom-call(s32[3]{0:T(128)S(1)} %copy-done.4, bf16[4,8,80,128]{3,2,1,0:T(8,128)(2,1)S(1)} %bitcast.4), custom_call_target="tpu_custom_call" | custom-call | tf_op jit(solution)/shard_map/pallas_call | solution.py:246
  32.9 20.8 %all_to_all.16.part_ref = bf16[64,3,128]{2,1,0:T(4,128)(2,1)S(1)} all-to-all(bf16[64,3,128]{2,1,0:T(4,128)(2,1)S(1)} %reshape.19), channel_id=1, replica_groups=mesh['b'=8,'a'=4,'chan'=8] {'b','chan'}, dimensions={0} | all-to-all | bytes 98304 | tf_op jit(solution)/shard_map/all_to_all | solution.py:336
  53.7 1.0 %shard_map.111 = bf16[32,24,128]{2,1,0:T(8,128)(2,1)} custom-call(bf16[64,3,128]{2,1,0:T(4,128)(2,1)S(1)} %all_to_all.16.part_ref), custom_call_target="tpu_custom_call" | custom-call | tf_op jit(solution)/shard_map/pallas_call | solution.py:283
  54.8 5.6 %all-to-all-start.2 = ((bf16[32,24,128]{2,1,0:T(8,128)(2,1)}), bf16[32,24,128]{2,1,0:T(8,128)(2,1)S(1)}, u32[]{:S(2)}, u32[]{:S(2)}) async-start(bf16[32,24,128]{2,1,0:T(8,128)(2,1)} %shard_map.111), calls=%async_computation.2 | async-start | bytes 393216 | tf_op jit(solution)/shard_map/all_to_all | solution.py:340
  60.4 10.4 %all-to-all-done.2.bins_ref = bf16[32,24,128]{2,1,0:T(8,128)(2,1)S(1)} async-done(((bf16[32,24,128]{2,1,0:T(8,128)(2,1)}), bf16[32,24,128]{2,1,0:T(8,128)(2,1)S(1)}, u32[]{:S(2)}, u32[]{:S(2)}) %all-to-all-start.2) | async-done | bytes 196640 | tf_op jit(solution)/shard_map/all_to_all | solution.py:340
  70.8 0.0 copy-done.2
  70.8 0.0 copy-done.3
  70.8 0.0 copy-done
  70.8 0.0 copy-done.1
  70.8 1.1 %shard_map.112 = f32[3,128,128]{2,1,0:T(8,128)} custom-call(s32[1]{0:T(128)} %bitcast.place_ref, bf16[32,24,128]{2,1,0:T(8,128)(2,1)S(1)} %all-to-all-done.2.bins_ref, f32[128,512]{1,0:T(8,128)S(1)} %copy-done.1, f32[128,512]{1,0:T(8,128)S(1)} %copy-done, f32[32,512]{1,0:T(8,128)S(1)} %copy-done.3, f32[32,512]{1,0:T(8,128)S(1)} %copy-done.2), custom_call_target="tpu_custom_call" | custom-call | tf_op jit(solution)/shard_map/pallas_call | solution.py:321
  (1 shorter events, 0.0 us)
Async XLA Ops:
  0.0 70.8 %copy-start.2 = (f32[32,512]{1,0:T(8,128)S(1)}, f32[32,512]{1,0:T(8,128)}, u32[]{:S(2)}) copy-start(f32[32,512]{1,0:T(8,128)} %constant.26.clone.second_ref) | copy-start | bytes 196612
  0.0 70.8 %copy-start.3 = (f32[32,512]{1,0:T(8,128)S(1)}, f32[32,512]{1,0:T(8,128)}, u32[]{:S(2)}) copy-start(f32[32,512]{1,0:T(8,128)} %constant.25.clone.first_ref) | copy-start | bytes 196612
  0.0 70.8 %copy-start = (f32[128,512]{1,0:T(8,128)S(1)}, f32[128,512]{1,0:T(8,128)}, u32[]{:S(2)}) copy-start(f32[128,512]{1,0:T(8,128)} %constant.24.clone.sin_ref) | copy-start | bytes 786436
  0.0 70.8 %copy-start.1 = (f32[128,512]{1,0:T(8,128)S(1)}, f32[128,512]{1,0:T(8,128)}, u32[]{:S(2)}) copy-start(f32[128,512]{1,0:T(8,128)} %constant.23.clone.cos_ref) | copy-start | bytes 786436
  0.0 27.6 %copy-start.4 = (s32[3]{0:T(128)S(1)}, s32[3]{0:T(128)}, u32[]{:S(2)}) copy-start(s32[3]{0:T(128)} %block_ref.1) | copy-start | bytes 40
  54.8 16.0 %all-to-all-start.2 = ((bf16[32,24,128]{2,1,0:T(8,128)(2,1)}), bf16[32,24,128]{2,1,0:T(8,128)(2,1)S(1)}, u32[]{:S(2)}, u32[]{:S(2)}) async-start(bf16[32,24,128]{2,1,0:T(8,128)(2,1)} %shard_map.111), calls=%async_computation.2 | async-start | bytes 393216 | tf_op jit(solution)/shard_map/all_to_all | solution.py:340

commit v4 on v3

--- a/solution.py
+++ b/solution.py
@@ -31,10 +31,7 @@
 ROWS = 2 * HALF
 META = 16
 QUARTERS = P_DEV // 128
-SUB = BIN_DEV // N_B
-TARGETS = N_B * N_CHAN
-KCOLS = N_CHAN * COLS
-PACKED = STEPS * SUB // 2
+OWNED = N_CHAN * COLS
 NT = (((1,), (1,)), ((), ()))
 BF = jnp.bfloat16
 F32 = jnp.float32
@@ -53,8 +50,8 @@
 
 
 def lag_tables():
-    shape = (N_A, 2, N_CHAN, 2, FG)
-    a, _, k, part, f = np.meshgrid(*[np.arange(n) for n in shape], indexing="ij")
+    shape = (N_A, N_CHAN, 2, FG)
+    a, k, part, f = np.meshgrid(*[np.arange(n) for n in shape], indexing="ij")
     freq = (FREQ0 + FG * (a * N_CHAN + k) + f).reshape(-1)
     part = part.reshape(-1)
     block = LAGS // N_WIN
@@ -90,25 +87,22 @@
         copy.wait()
 
     slots = slot_ref[...]
-    owner, low = slots // BIN_DEV, slots % BIN_DEV
-    target = low // 8 % N_B * N_CHAN + owner
-    sub = low // 64 * 8 + low % 8
-    tables = jnp.concatenate([target, sub], axis=0).astype(F32).astype(BF)
+    tables = jnp.concatenate([slots % BIN_DEV, slots // BIN_DEV], axis=0).astype(F32).astype(BF)
     lane = lax.broadcasted_iota(jnp.int32, (128, P_DEV), 0)
     high = lax.broadcasted_iota(jnp.int32, (8, P_DEV), 0)
-    place = place_ref[0]
+    place = place_ref[0] % N_A
     pieces = []
     for s in range(STEPS):
         bins = bin_ref[s : s + 1, :]
         onehot = jnp.where(lane == bins % 128, 1.0, 0.0).astype(BF)
         found = jnp.dot(tables, onehot, preferred_element_type=F32)
         here = high == bins // 128
-        targets = jnp.sum(jnp.where(here, found[:8], 0.0), axis=0, keepdims=True)
-        subs = jnp.sum(jnp.where(here, found[8:], 0.0), axis=0, keepdims=True)
+        row_in_owner = jnp.sum(jnp.where(here, found[:8], 0.0), axis=0, keepdims=True)
+        owner = jnp.sum(jnp.where(here, found[8:], 0.0), axis=0, keepdims=True)
         row = jnp.where(
             place < 2,
             jnp.where(place == 0, source_ref[s : s + 1, :], receiver_ref[s : s + 1, :]).astype(F32),
-            jnp.where(place == 2, targets, subs),
+            jnp.where(place == 2, row_in_owner, owner),
         )
         pieces += [row[:, q * 128 : (q + 1) * 128] for q in range(QUARTERS)]
     pieces.append(jnp.zeros((META - len(pieces), 128), F32))
@@ -183,18 +177,18 @@
     )
 
 
-def pairs_kernel(block_ref, y_ref, out_ref, source_ref, placed_ref, target_ref):
+def pairs_kernel(block_ref, y_ref, out_ref, source_ref, placed_ref, row_ref):
     index = lax.broadcasted_iota(jnp.int32, (128, 128), 0).astype(F32).astype(BF)
     low_half = lax.broadcasted_iota(jnp.int32, (8, P_DEV), 0) < FG
     lower_row = (lax.broadcasted_iota(jnp.int32, (16, 128), 0) // 8).astype(F32)
     one, zero = jnp.ones((), BF), jnp.zeros((), BF)
 
-    def spread(row, count):
+    def spread(row):
         columns = []
         for q in range(QUARTERS):
             entry = jnp.broadcast_to(row[q : q + 1], (16, 128)).astype(BF)
-            entry = jnp.concatenate([entry] * (count // 16), axis=0)
-            columns.append(jnp.where(index[:count] == entry, one, zero))
+            entry = jnp.concatenate([entry] * 8, axis=0)
+            columns.append(jnp.where(index == entry, one, zero))
         return jnp.concatenate(columns, axis=1)
 
     for s in range(STEPS):
@@ -208,8 +202,8 @@
                 for kind in range(4)
             ]
             receiver = jnp.concatenate([y_ref[a, c, :ROWS, :] for a in range(N_A)], axis=0)
-            u = jnp.dot(source_ref[...], spread(lists[0], CH_DEV), preferred_element_type=F32)
-            v = jnp.dot(receiver, spread(lists[1], CH_DEV), preferred_element_type=F32)
+            u = jnp.dot(source_ref[...], spread(lists[0]), preferred_element_type=F32)
+            v = jnp.dot(receiver, spread(lists[1]), preferred_element_type=F32)
             real_part = jnp.zeros((8, P_DEV), F32)
             imag_part = jnp.zeros((8, P_DEV), F32)
             for a in range(N_A):
@@ -224,22 +218,22 @@
             partial = jnp.where(low_half, real_part, imag_part)
             partial = jnp.concatenate([partial, partial], axis=0).astype(BF)
             for q in range(QUARTERS):
-                sub = (jnp.broadcast_to(lists[3][q : q + 1], (16, 128)) - lower_row).astype(BF)
+                owner = (jnp.broadcast_to(lists[3][q : q + 1], (16, 128)) - lower_row).astype(BF)
                 values = partial[:, q * 128 : (q + 1) * 128]
                 lanes = pl.ds(pl.multiple_of(c * P_DEV + q * 128, 128), 128)
-                for k in range(0, SUB, 2):
+                for k in range(0, N_CHAN, 2):
                     placed_ref[k * 8 : k * 8 + 16, lanes] = jnp.where(
-                        sub == jnp.full((16, 128), float(k), BF), values, zero
+                        owner == jnp.full((16, 128), float(k), BF), values, zero
                     )
-            target_ref[:, pl.ds(pl.multiple_of(c * P_DEV, 128), P_DEV)] = spread(
-                lists[2], TARGETS
-            )
+            row_ref[:, pl.ds(pl.multiple_of(c * P_DEV, 128), P_DEV)] = spread(lists[2])
             return carry
 
         lax.fori_loop(0, N_CHAN, body, 0, unroll=8)
-        out_ref[:, s * 128 : (s + 1) * 128] = lax.dot_general(
-            target_ref[...], placed_ref[...], NT, preferred_element_type=F32
+        binned = lax.dot_general(
+            placed_ref[...], row_ref[...], NT, preferred_element_type=F32
         ).astype(BF)
+        for b in range(N_B):
+            out_ref[b, :, s * BIN_DEV : (s + 1) * BIN_DEV] = binned
 
 
 def bin_pairs(source_block, chunks):
@@ -247,36 +241,23 @@
         pairs_kernel,
         in_specs=[SMEM, VMEM],
         out_specs=VMEM,
-        out_shape=jax.ShapeDtypeStruct((TARGETS, STEPS * SUB * COLS), BF),
+        out_shape=jax.ShapeDtypeStruct((N_B, OWNED, STEPS * BIN_DEV), BF),
         scratch_shapes=[
             pltpu.VMEM((N_A * ROWS, CH_DEV), BF),
-            pltpu.VMEM((SUB * COLS, N_CHAN * P_DEV), BF),
-            pltpu.VMEM((TARGETS, N_CHAN * P_DEV), BF),
+            pltpu.VMEM((OWNED, N_CHAN * P_DEV), BF),
+            pltpu.VMEM((BIN_DEV, N_CHAN * P_DEV), BF),
         ],
         compiler_params=pltpu.CompilerParams(vmem_limit_bytes=32 << 20),
     )(source_block, chunks)
 
 
 def sum_kernel(part_ref, out_ref):
-    parts = part_ref[...].astype(F32).reshape(N_B, N_CHAN, STEPS, 128)
-    total = jnp.sum(parts, axis=0).astype(BF).astype(F32)
-    lane = lax.broadcasted_iota(jnp.int32, (SUB, 128), 1)
-    here = lane // COLS == lax.broadcasted_iota(jnp.int32, (SUB, 128), 0)
-    wide = []
-    for k in range(N_CHAN):
-        rows = [
-            jnp.where(here, total[k, s : s + 1], 0.0) for s in range(STEPS)
-        ]
-        wide.append(jnp.concatenate(rows, axis=0).astype(BF))
-    wide = jnp.concatenate(wide, axis=1)
-    row = lax.broadcasted_iota(jnp.int32, (N_CHAN * 128, KCOLS), 0)
-    column = lax.broadcasted_iota(jnp.int32, (N_CHAN * 128, KCOLS), 1)
-    fold = (row % COLS == column % COLS) & (row // 128 == column // COLS)
-    fold = jnp.where(fold, 1.0, 0.0).astype(BF)
-    packed = jnp.dot(wide, fold, preferred_element_type=F32)
-    packed = jnp.concatenate([packed[:PACKED], packed[PACKED:]], axis=1).astype(BF)
-    for w in range(N_WIN):
-        out_ref[w] = packed
+    total = part_ref[0].astype(F32)
+    for b in range(1, N_B):
+        total += part_ref[b].astype(F32)
+    total = total.astype(BF)
+    for a in range(N_A):
+        out_ref[a] = total
 
 
 def sum_windows(parts):
@@ -284,7 +265,7 @@
         sum_kernel,
         in_specs=[VMEM],
         out_specs=VMEM,
-        out_shape=jax.ShapeDtypeStruct((N_WIN, PACKED, 128), BF),
+        out_shape=jax.ShapeDtypeStruct((N_A, OWNED, STEPS * BIN_DEV), BF),
         compiler_params=pltpu.CompilerParams(vmem_limit_bytes=8 << 20),
     )(parts)
 
@@ -297,24 +278,12 @@
     )
     upper = basis.astype(BF)
     rest = (basis - upper.astype(F32)).astype(BF)
-    lane_half = lax.broadcasted_iota(jnp.int32, (64, 128), 1) // KCOLS
+    bins = bins_ref[...]
+    stacks = jnp.dot(upper, bins, preferred_element_type=F32) + jnp.dot(
+        rest, bins, preferred_element_type=F32
+    )
     for s in range(STEPS):
-        pieces = []
-        for part in range(2):
-            first = s * SUB + part * 8
-            half, at = first // PACKED, first % PACKED
-            columns = []
-            for a in range(N_A):
-                rows = [
-                    bins_ref[b * N_A + a].astype(F32)[at : at + 8] for b in range(N_B)
-                ]
-                rows = jnp.concatenate(rows, axis=0)
-                columns.append(jnp.where(lane_half == half, rows, 0.0).astype(BF))
-            pieces.append(jnp.concatenate(columns, axis=1))
-        binned = jnp.concatenate(pieces, axis=0)
-        out_ref[s] = lax.dot_general(
-            upper, binned, NT, preferred_element_type=F32
-        ) + lax.dot_general(rest, binned, NT, preferred_element_type=F32)
+        out_ref[s] = stacks[:, s * BIN_DEV : (s + 1) * BIN_DEV]
 
 
 def project_lags(place, bins):
@@ -323,22 +292,19 @@
         in_specs=[SMEM] + [VMEM] * 5,
         out_specs=VMEM,
         out_shape=jax.ShapeDtypeStruct((STEPS, LAGS // N_WIN, BIN_DEV), F32),
-        compiler_params=pltpu.CompilerParams(vmem_limit_bytes=32 << 20),
+        compiler_params=pltpu.CompilerParams(vmem_limit_bytes=16 << 20),
     )(place, bins, *[jnp.asarray(t) for t in lag_tables()])
 
 
 def on_device(traces, source_block, pair_source, pair_receiver, pair_bin, bin_slot):
-    place_a = lax.axis_index("a").reshape(1)
-    place_win = lax.axis_index(("b", "a")).reshape(1)
-    chunks = whiten(place_a, traces, pair_source, pair_receiver, pair_bin, bin_slot)
+    place = lax.axis_index(("b", "a")).reshape(1)
+    chunks = whiten(place, traces, pair_source, pair_receiver, pair_bin, bin_slot)
     chunks = lax.all_to_all(chunks, ("a", "chan"), 0, 0, tiled=True)
     parts = bin_pairs(source_block, chunks.reshape(N_A, N_CHAN, ROWS + META, CH_DEV))
-    parts = lax.all_to_all(
-        parts.reshape(TARGETS, STEPS, 128), ("b", "chan"), 0, 0, tiled=True
-    )
-    bins = sum_windows(parts)
-    bins = lax.all_to_all(bins, ("b", "a"), 0, 0, tiled=True)
-    return project_lags(place_win, bins)
+    parts = lax.all_to_all(parts, "b", 0, 0, tiled=True)
+    bins = sum_windows(parts).reshape(GROUPS, COLS, STEPS * BIN_DEV)
+    bins = lax.all_to_all(bins, ("a", "chan"), 0, 0, tiled=True)
+    return project_lags(place, bins.reshape(2 * F, STEPS * BIN_DEV))
 
 
 def solution(mesh):

time: 72.1 us -> 69 us (0.957)
  blocking collectives: 42.5 us -> 56.6 us
  waiting for transfers between devices: 10.4 us -> 0 us
  starting transfers between devices: 5.64 us -> 0 us
  Pallas kernels: 13.2 us -> 12.1 us
    all_to_all x1 -> x2, blocking collectives: 20.8 us -> 34.9 us  [the longest x1 23.2 us: on_device(): parts = lax.all_to_all(parts, 'b', 0, 0, tiled=True)]
    all_to_all x1 -> x0, waiting for transfers between devices: 10.4 us -> none  [on_device(): bins = lax.all_to_all(bins, ('b', 'a'), 0, 0, tiled=True)]
    all_to_all x1 -> x0, starting transfers between devices: 5.64 us -> none  [on_device(): bins = lax.all_to_all(bins, ('b', 'a'), 0, 0, tiled=True)]
    pallas_call x1, Pallas kernels: 1.04 us -> 0.06 us  [sum_windows(): pl.pallas_call(sum_kernel, in_specs=[VMEM], out_specs=VMEM, out_shape=jax...]
  transfers between devices with their start and end apart: 1 -> 0, of which waited for: 1 -> 0; matrix products, arithmetic and copies ran while one was open for 0% -> 0% of each run, Pallas kernels for 0% -> 0%
where the time goes in v4:
time: 69 us; the launch traced here: 68.8 us
  blocking collectives  56.6 us (82%)
  Pallas kernels  12.1 us (18%)
    all_to_all x1, blocking collectives, on_device(): parts = lax.all_to_all(parts, 'b', 0, 0, tiled=True)  23.2 us
    all_to_all x1, blocking collectives, on_device(): chunks = lax.all_to_all(chunks, ('a', 'chan'), 0, 0, tiled=True)  21.7 us
    all_to_all x1, blocking collectives, on_device(): bins = lax.all_to_all(bins, ('a', 'chan'), 0, 0, tiled=True)  11.7 us
    pallas_call x1, Pallas kernels, whiten(): pl.pallas_call(whiten_kernel, in_specs=[SMEM] + [HBM] * 6, out_specs=VMEM...  5.82 us
    pallas_call x1, Pallas kernels, bin_pairs(): pl.pallas_call(pairs_kernel, in_specs=[SMEM, VMEM], out_specs=VMEM, out_s...  5.31 us

profile of v4, /device:TPU:1, one launch (start us, length us, event | category | flops | bytes accessed | tf_op | source)
XLA Modules:
  0.0 68.8 jit_solution(9312316820190589484)
XLA Ops:
  0.0 0.0 copy-start.2
  0.0 0.0 copy-start.3
  0.0 0.0 copy-start
  0.0 0.0 copy-start.1
  0.0 0.0 copy-start.4
  0.0 5.8 %shard_map.109 = bf16[32,80,128]{2,1,0:T(8,128)(2,1)S(1)} custom-call(s32[1]{0:T(128)} %bitcast.place_ref, bf16[8,128,4096]{2,1,0:T(8,128)(2,1)} %x_hbm.1, f32[128,384]{1,0:T(8,128)} %constant.22.clone.basis_hbm, s32[8,128]{1,0:T(8,128)} %bitcast.8, s32[3,512]{1,0:T(4,128)} %source_hbm.1, s32[3,512]{1,0:T(4,128)} %receiver_hbm.1, s32[3,512]{1,0:T(4,128)} %bin_hbm.1), custom_call_target="tpu_custom_call" | custom-call | tf_op jit(solution)/shard_map/pallas_call | solution.py:150
  5.9 21.7 %all_to_all.15 = bf16[32,80,128]{2,1,0:T(8,128)(2,1)S(1)} all-to-all(bf16[32,80,128]{2,1,0:T(8,128)(2,1)S(1)} %shard_map.109), channel_id=1, replica_groups=mesh['b'=8,'a'=4,'chan'=8] {'a','chan'}, dimensions={0} | all-to-all | bytes 1310720 | tf_op jit(solution)/shard_map/all_to_all | solution.py:302
  27.6 0.0 copy-done.4
  27.6 5.3 %shard_map.110 = bf16[8,64,384]{2,1,0:T(8,128)(2,1)S(1)} custom-call(s32[3]{0:T(128)S(1)} %copy-done.4, bf16[4,8,80,128]{3,2,1,0:T(8,128)(2,1)S(1)} %bitcast.5), custom_call_target="tpu_custom_call" | custom-call | tf_op jit(solution)/shard_map/pallas_call | solution.py:240
  32.9 23.2 %all_to_all.16.part_ref = bf16[8,64,384]{2,1,0:T(8,128)(2,1)S(1)} all-to-all(bf16[8,64,384]{2,1,0:T(8,128)(2,1)S(1)} %shard_map.110), channel_id=1, replica_groups=mesh['b'=8,'a'=4,'chan'=8] {'b'}, dimensions={0} | all-to-all | bytes 786432 | tf_op jit(solution)/shard_map/all_to_all | solution.py:304
  56.1 0.1 shard_map.111
  56.2 11.7 %all_to_all.17 = bf16[32,8,384]{2,1,0:T(8,128)(2,1)S(1)} all-to-all(bf16[32,8,384]{2,1,0:T(8,128)(2,1)S(1)} %bitcast.7), channel_id=1, replica_groups=mesh['b'=8,'a'=4,'chan'=8] {'a','chan'}, dimensions={0} | all-to-all | bytes 393216 | tf_op jit(solution)/shard_map/all_to_all | solution.py:306
  67.9 0.0 copy-done.2
  67.9 0.0 copy-done.3
  67.9 0.0 copy-done
  67.9 0.0 copy-done.1
  67.9 0.9 %shard_map.112 = f32[3,128,128]{2,1,0:T(8,128)} custom-call(s32[1]{0:T(128)} %bitcast.place_ref, bf16[256,384]{1,0:T(8,128)(2,1)S(1)} %bitcast.6, f32[128,256]{1,0:T(8,128)S(1)} %copy-done.1, f32[128,256]{1,0:T(8,128)S(1)} %copy-done, f32[32,256]{1,0:T(8,128)S(1)} %copy-done.3, f32[32,256]{1,0:T(8,128)S(1)} %copy-done.2), custom_call_target="tpu_custom_call" | custom-call | tf_op jit(solution)/shard_map/pallas_call | solution.py:290
Async XLA Ops:
  0.0 67.9 %copy-start.2 = (f32[32,256]{1,0:T(8,128)S(1)}, f32[32,256]{1,0:T(8,128)}, u32[]{:S(2)}) copy-start(f32[32,256]{1,0:T(8,128)} %constant.26.clone.second_ref) | copy-start | bytes 98308
  0.0 67.9 %copy-start.3 = (f32[32,256]{1,0:T(8,128)S(1)}, f32[32,256]{1,0:T(8,128)}, u32[]{:S(2)}) copy-start(f32[32,256]{1,0:T(8,128)} %constant.25.clone.first_ref) | copy-start | bytes 98308
  0.0 67.9 %copy-start = (f32[128,256]{1,0:T(8,128)S(1)}, f32[128,256]{1,0:T(8,128)}, u32[]{:S(2)}) copy-start(f32[128,256]{1,0:T(8,128)} %constant.24.clone.sin_ref) | copy-start | bytes 393220
  0.0 67.9 %copy-start.1 = (f32[128,256]{1,0:T(8,128)S(1)}, f32[128,256]{1,0:T(8,128)}, u32[]{:S(2)}) copy-start(f32[128,256]{1,0:T(8,128)} %constant.23.clone.cos_ref) | copy-start | bytes 393220
  0.0 27.6 %copy-start.4 = (s32[3]{0:T(128)S(1)}, s32[3]{0:T(128)}, u32[]{:S(2)}) copy-start(s32[3]{0:T(128)} %block_ref.1) | copy-start | bytes 40

commit v5 on v4

--- a/solution.py
+++ b/solution.py
@@ -81,50 +81,54 @@
         pltpu.make_async_copy(x_hbm.at[pl.ds(2 * i, 2)], x_ref.at[pl.ds(2 * i, 2)], x_sem.at[i])
         for i in range(WIN_DEV // 2)
     ]
-    for copy in small + x_copies[:2]:
+    for copy in small[-1:] + x_copies[:2] + small[:-1]:
         copy.start()
-    for copy in small:
-        copy.wait()
-
-    slots = slot_ref[...]
-    tables = jnp.concatenate([slots % BIN_DEV, slots // BIN_DEV], axis=0).astype(F32).astype(BF)
-    lane = lax.broadcasted_iota(jnp.int32, (128, P_DEV), 0)
-    high = lax.broadcasted_iota(jnp.int32, (8, P_DEV), 0)
-    place = place_ref[0] % N_A
-    pieces = []
-    for s in range(STEPS):
-        bins = bin_ref[s : s + 1, :]
-        onehot = jnp.where(lane == bins % 128, 1.0, 0.0).astype(BF)
-        found = jnp.dot(tables, onehot, preferred_element_type=F32)
-        here = high == bins // 128
-        row_in_owner = jnp.sum(jnp.where(here, found[:8], 0.0), axis=0, keepdims=True)
-        owner = jnp.sum(jnp.where(here, found[8:], 0.0), axis=0, keepdims=True)
-        row = jnp.where(
-            place < 2,
-            jnp.where(place == 0, source_ref[s : s + 1, :], receiver_ref[s : s + 1, :]).astype(F32),
-            jnp.where(place == 2, row_in_owner, owner),
-        )
-        pieces += [row[:, q * 128 : (q + 1) * 128] for q in range(QUARTERS)]
-    pieces.append(jnp.zeros((META - len(pieces), 128), F32))
-    block = jnp.concatenate(pieces, axis=0).astype(BF)
-    for group in range(GROUPS):
-        out_ref[group, ROWS:, :] = block
-
-    for copy in x_copies[2:]:
-        copy.start()
+    small[-1].wait()
     cos_in, sin_in = basis_ref[:, :128], basis_ref[:, 128:256]
     starts = WLEN // 128
     for q in range(starts):
+        if q == starts // 2:
+            for copy in x_copies[2:]:
+                copy.start()
         cos_out = jnp.broadcast_to(basis_ref[:, 256 + q : 257 + q], (F, 128))
         sin_out = jnp.broadcast_to(basis_ref[:, 256 + starts + q : 257 + starts + q], (F, 128))
         lanes = slice(q * 128, (q + 1) * 128)
         table_ref[:F, lanes] = (cos_out * cos_in - sin_out * sin_in).astype(BF)
         table_ref[F:, lanes] = (-(sin_out * cos_in) - cos_out * sin_in).astype(BF)
+    def write_lists():
+        slots = slot_ref[...]
+        tables = jnp.concatenate([slots % BIN_DEV, slots // BIN_DEV], axis=0).astype(F32).astype(BF)
+        lane = lax.broadcasted_iota(jnp.int32, (128, P_DEV), 0)
+        high = lax.broadcasted_iota(jnp.int32, (8, P_DEV), 0)
+        place = place_ref[0] % N_A
+        pieces = []
+        for s in range(STEPS):
+            bins = bin_ref[s : s + 1, :]
+            onehot = jnp.where(lane == bins % 128, 1.0, 0.0).astype(BF)
+            found = jnp.dot(tables, onehot, preferred_element_type=F32)
+            here = high == bins // 128
+            row_in_owner = jnp.sum(jnp.where(here, found[:8], 0.0), axis=0, keepdims=True)
+            owner = jnp.sum(jnp.where(here, found[8:], 0.0), axis=0, keepdims=True)
+            row = jnp.where(
+                place < 2,
+                jnp.where(place == 0, source_ref[s : s + 1, :], receiver_ref[s : s + 1, :]).astype(F32),
+                jnp.where(place == 2, row_in_owner, owner),
+            )
+            pieces += [row[:, q * 128 : (q + 1) * 128] for q in range(QUARTERS)]
+        pieces.append(jnp.zeros((META - len(pieces), 128), F32))
+        block = jnp.concatenate(pieces, axis=0).astype(BF)
+        for group in range(GROUPS):
+            out_ref[group, ROWS:, :] = block
+
     upper = lax.broadcasted_iota(jnp.int32, (1, 8, 128), 1) < FG
     for i in range(WIN_DEV // 2):
         if i % 2 == 0:
             x_copies[i].wait()
             x_copies[i + 1].wait()
+        if i == 0:
+            for copy in small[:-1]:
+                copy.wait()
+            write_lists()
         rows = x_ref[2 * i : 2 * i + 2].reshape(2 * CH_DEV, WLEN)
         spectra = lax.dot_general(table_ref[...], rows, NT, preferred_element_type=F32)
         power = jnp.sum(spectra * spectra, axis=0, keepdims=True) * (1.0 / (2 * F))

time: 69 us -> 68.6 us (level)
  no operation moved by 1% of the time
where the time goes in v5:
time: 68.6 us; the launch traced here: 68.5 us
  blocking collectives  56.6 us (83%)
  Pallas kernels  11.8 us (17%)
    all_to_all x1, blocking collectives, on_device(): parts = lax.all_to_all(parts, 'b', 0, 0, tiled=True)  23.2 us
    all_to_all x1, blocking collectives, on_device(): chunks = lax.all_to_all(chunks, ('a', 'chan'), 0, 0, tiled=True)  21.8 us
    all_to_all x1, blocking collectives, on_device(): bins = lax.all_to_all(bins, ('a', 'chan'), 0, 0, tiled=True)  11.7 us
    pallas_call x1, Pallas kernels, whiten(): pl.pallas_call(whiten_kernel, in_specs=[SMEM] + [HBM] * 6, out_specs=VMEM...  5.49 us
    pallas_call x1, Pallas kernels, bin_pairs(): pl.pallas_call(pairs_kernel, in_specs=[SMEM, VMEM], out_specs=VMEM, out_s...  5.31 us

profile of v5, /device:TPU:1, one launch (start us, length us, event | category | flops | bytes accessed | tf_op | source)
XLA Modules:
  0.0 68.5 jit_solution(12265336975829270440)
XLA Ops:
  0.0 0.0 copy-start.2
  0.0 0.0 copy-start.3
  0.0 0.0 copy-start
  0.0 0.0 copy-start.1
  0.0 0.0 copy-start.4
  0.0 5.5 %shard_map.109 = bf16[32,80,128]{2,1,0:T(8,128)(2,1)S(1)} custom-call(s32[1]{0:T(128)} %bitcast.place_ref, bf16[8,128,4096]{2,1,0:T(8,128)(2,1)} %x_hbm.1, f32[128,384]{1,0:T(8,128)} %constant.22.clone.basis_hbm, s32[8,128]{1,0:T(8,128)} %bitcast.8, s32[3,512]{1,0:T(4,128)} %source_hbm.1, s32[3,512]{1,0:T(4,128)} %receiver_hbm.1, s32[3,512]{1,0:T(4,128)} %bin_hbm.1), custom_call_target="tpu_custom_call" | custom-call | tf_op jit(solution)/shard_map/pallas_call | solution.py:154
  5.5 21.8 %all_to_all.15 = bf16[32,80,128]{2,1,0:T(8,128)(2,1)S(1)} all-to-all(bf16[32,80,128]{2,1,0:T(8,128)(2,1)S(1)} %shard_map.109), channel_id=1, replica_groups=mesh['b'=8,'a'=4,'chan'=8] {'a','chan'}, dimensions={0} | all-to-all | bytes 1310720 | tf_op jit(solution)/shard_map/all_to_all | solution.py:306
  27.3 0.0 copy-done.4
  27.3 5.3 %shard_map.110 = bf16[8,64,384]{2,1,0:T(8,128)(2,1)S(1)} custom-call(s32[3]{0:T(128)S(1)} %copy-done.4, bf16[4,8,80,128]{3,2,1,0:T(8,128)(2,1)S(1)} %bitcast.5), custom_call_target="tpu_custom_call" | custom-call | tf_op jit(solution)/shard_map/pallas_call | solution.py:244
  32.6 23.2 %all_to_all.16.part_ref = bf16[8,64,384]{2,1,0:T(8,128)(2,1)S(1)} all-to-all(bf16[8,64,384]{2,1,0:T(8,128)(2,1)S(1)} %shard_map.110), channel_id=1, replica_groups=mesh['b'=8,'a'=4,'chan'=8] {'b'}, dimensions={0} | all-to-all | bytes 786432 | tf_op jit(solution)/shard_map/all_to_all | solution.py:308
  55.8 0.1 shard_map.111
  55.8 11.7 %all_to_all.17 = bf16[32,8,384]{2,1,0:T(8,128)(2,1)S(1)} all-to-all(bf16[32,8,384]{2,1,0:T(8,128)(2,1)S(1)} %bitcast.7), channel_id=1, replica_groups=mesh['b'=8,'a'=4,'chan'=8] {'a','chan'}, dimensions={0} | all-to-all | bytes 393216 | tf_op jit(solution)/shard_map/all_to_all | solution.py:310
  67.5 0.0 copy-done.2
  67.5 0.0 copy-done.3
  67.5 0.0 copy-done
  67.5 0.0 copy-done.1
  67.6 0.9 %shard_map.112 = f32[3,128,128]{2,1,0:T(8,128)} custom-call(s32[1]{0:T(128)} %bitcast.place_ref, bf16[256,384]{1,0:T(8,128)(2,1)S(1)} %bitcast.6, f32[128,256]{1,0:T(8,128)S(1)} %copy-done.1, f32[128,256]{1,0:T(8,128)S(1)} %copy-done, f32[32,256]{1,0:T(8,128)S(1)} %copy-done.3, f32[32,256]{1,0:T(8,128)S(1)} %copy-done.2), custom_call_target="tpu_custom_call" | custom-call | tf_op jit(solution)/shard_map/pallas_call | solution.py:294
Async XLA Ops:
  0.0 67.5 %copy-start.2 = (f32[32,256]{1,0:T(8,128)S(1)}, f32[32,256]{1,0:T(8,128)}, u32[]{:S(2)}) copy-start(f32[32,256]{1,0:T(8,128)} %constant.26.clone.second_ref) | copy-start | bytes 98308
  0.0 67.5 %copy-start.3 = (f32[32,256]{1,0:T(8,128)S(1)}, f32[32,256]{1,0:T(8,128)}, u32[]{:S(2)}) copy-start(f32[32,256]{1,0:T(8,128)} %constant.25.clone.first_ref) | copy-start | bytes 98308
  0.0 67.5 %copy-start = (f32[128,256]{1,0:T(8,128)S(1)}, f32[128,256]{1,0:T(8,128)}, u32[]{:S(2)}) copy-start(f32[128,256]{1,0:T(8,128)} %constant.24.clone.sin_ref) | copy-start | bytes 393220
  0.0 67.5 %copy-start.1 = (f32[128,256]{1,0:T(8,128)S(1)}, f32[128,256]{1,0:T(8,128)}, u32[]{:S(2)}) copy-start(f32[128,256]{1,0:T(8,128)} %constant.23.clone.cos_ref) | copy-start | bytes 393220
  0.0 27.3 %copy-start.4 = (s32[3]{0:T(128)S(1)}, s32[3]{0:T(128)}, u32[]{:S(2)}) copy-start(s32[3]{0:T(128)} %block_ref.1) | copy-start | bytes 40

commit v6 on v5

--- a/solution.py
+++ b/solution.py
@@ -29,6 +29,7 @@
 COLS = 2 * FG
 HALF = WIN_DEV * FG
 ROWS = 2 * HALF
+GROUPQ = 2
 META = 16
 QUARTERS = P_DEV // 128
 OWNED = N_CHAN * COLS
@@ -189,7 +190,7 @@
 
     def spread(row):
         columns = []
-        for q in range(QUARTERS):
+        for q in range(row.shape[0]):
             entry = jnp.broadcast_to(row[q : q + 1], (16, 128)).astype(BF)
             entry = jnp.concatenate([entry] * 8, axis=0)
             columns.append(jnp.where(index == entry, one, zero))
@@ -206,20 +207,28 @@
                 for kind in range(4)
             ]
             receiver = jnp.concatenate([y_ref[a, c, :ROWS, :] for a in range(N_A)], axis=0)
-            u = jnp.dot(source_ref[...], spread(lists[0]), preferred_element_type=F32)
-            v = jnp.dot(receiver, spread(lists[1]), preferred_element_type=F32)
-            real_part = jnp.zeros((8, P_DEV), F32)
-            imag_part = jnp.zeros((8, P_DEV), F32)
-            for a in range(N_A):
-                for r in range(0, HALF, 8):
-                    at = a * ROWS + r
-                    u_re, u_im = u[at : at + 8], u[at + HALF : at + HALF + 8]
-                    v_re, v_im = v[at : at + 8], v[at + HALF : at + HALF + 8]
-                    real_part += u_re * v_re + u_im * v_im
-                    imag_part += u_re * v_im - u_im * v_re
-            real_part += pltpu.roll(real_part, FG, axis=0)
-            imag_part += pltpu.roll(imag_part, FG, axis=0)
-            partial = jnp.where(low_half, real_part, imag_part)
+            pieces = []
+            for q in range(0, QUARTERS, GROUPQ):
+                width = GROUPQ * 128
+                u = jnp.dot(
+                    source_ref[...], spread(lists[0][q : q + GROUPQ]), preferred_element_type=F32
+                )
+                v = jnp.dot(
+                    receiver, spread(lists[1][q : q + GROUPQ]), preferred_element_type=F32
+                )
+                real_part = jnp.zeros((8, width), F32)
+                imag_part = jnp.zeros((8, width), F32)
+                for a in range(N_A):
+                    for r in range(0, HALF, 8):
+                        at = a * ROWS + r
+                        u_re, u_im = u[at : at + 8], u[at + HALF : at + HALF + 8]
+                        v_re, v_im = v[at : at + 8], v[at + HALF : at + HALF + 8]
+                        real_part += u_re * v_re + u_im * v_im
+                        imag_part += u_re * v_im - u_im * v_re
+                real_part += pltpu.roll(real_part, FG, axis=0)
+                imag_part += pltpu.roll(imag_part, FG, axis=0)
+                pieces.append(jnp.where(low_half[:, :width], real_part, imag_part))
+            partial = jnp.concatenate(pieces, axis=1)
             partial = jnp.concatenate([partial, partial], axis=0).astype(BF)
             for q in range(QUARTERS):
                 owner = (jnp.broadcast_to(lists[3][q : q + 1], (16, 128)) - lower_row).astype(BF)
@@ -274,7 +283,7 @@
     )(parts)
 
 
-def lag_kernel(place_ref, bins_ref, cos_ref, sin_ref, first_ref, second_ref, out_ref):
+def lag_kernel(place_ref, bins_ref, cos_ref, sin_ref, first_ref, second_ref, out_hbm, out_ref, sem):
     place = place_ref[0]
     basis = (
         cos_ref[...] * first_ref[pl.ds(place, 1), :]
@@ -282,20 +291,28 @@
     )
     upper = basis.astype(BF)
     rest = (basis - upper.astype(F32)).astype(BF)
-    bins = bins_ref[...]
-    stacks = jnp.dot(upper, bins, preferred_element_type=F32) + jnp.dot(
-        rest, bins, preferred_element_type=F32
-    )
+    copies = []
     for s in range(STEPS):
-        out_ref[s] = stacks[:, s * BIN_DEV : (s + 1) * BIN_DEV]
+        bins = bins_ref[:, s * BIN_DEV : (s + 1) * BIN_DEV]
+        out_ref[s] = jnp.dot(upper, bins, preferred_element_type=F32) + jnp.dot(
+            rest, bins, preferred_element_type=F32
+        )
+        copies.append(pltpu.make_async_copy(out_ref.at[s], out_hbm.at[s], sem.at[s]))
+        copies[s].start()
+    for copy in copies:
+        copy.wait()
 
 
 def project_lags(place, bins):
     return pl.pallas_call(
         lag_kernel,
         in_specs=[SMEM] + [VMEM] * 5,
-        out_specs=VMEM,
+        out_specs=HBM,
         out_shape=jax.ShapeDtypeStruct((STEPS, LAGS // N_WIN, BIN_DEV), F32),
+        scratch_shapes=[
+            pltpu.VMEM((STEPS, LAGS // N_WIN, BIN_DEV), F32),
+            pltpu.SemaphoreType.DMA((STEPS,)),
+        ],
         compiler_params=pltpu.CompilerParams(vmem_limit_bytes=16 << 20),
     )(place, bins, *[jnp.asarray(t) for t in lag_tables()])
 

time: 68.6 us -> 68.6 us (level)
  no operation moved by 1% of the time
where the time goes in v6:
time: 68.6 us; the launch traced here: 68.4 us
  blocking collectives  56.6 us (83%)
  Pallas kernels  11.7 us (17%)
    all_to_all x1, blocking collectives, on_device(): parts = lax.all_to_all(parts, 'b', 0, 0, tiled=True)  23.2 us
    all_to_all x1, blocking collectives, on_device(): chunks = lax.all_to_all(chunks, ('a', 'chan'), 0, 0, tiled=True)  21.8 us
    all_to_all x1, blocking collectives, on_device(): bins = lax.all_to_all(bins, ('a', 'chan'), 0, 0, tiled=True)  11.7 us
    pallas_call x1, Pallas kernels, whiten(): pl.pallas_call(whiten_kernel, in_specs=[SMEM] + [HBM] * 6, out_specs=VMEM...  5.49 us
    pallas_call x1, Pallas kernels, bin_pairs(): pl.pallas_call(pairs_kernel, in_specs=[SMEM, VMEM], out_specs=VMEM, out_s...  5.24 us

profile of v6, /device:TPU:1, one launch (start us, length us, event | category | flops | bytes accessed | tf_op | source)
XLA Modules:
  0.0 68.4 jit_solution(16944625880479489550)
XLA Ops:
  0.0 0.0 copy-start.2
  0.0 0.0 copy-start.3
  0.0 0.0 copy-start
  0.0 0.0 copy-start.1
  0.0 0.0 copy-start.4
  0.0 5.5 %shard_map.109 = bf16[32,80,128]{2,1,0:T(8,128)(2,1)S(1)} custom-call(s32[1]{0:T(128)} %bitcast.place_ref, bf16[8,128,4096]{2,1,0:T(8,128)(2,1)} %x_hbm.1, f32[128,384]{1,0:T(8,128)} %constant.22.clone.basis_hbm, s32[8,128]{1,0:T(8,128)} %bitcast.8, s32[3,512]{1,0:T(4,128)} %source_hbm.1, s32[3,512]{1,0:T(4,128)} %receiver_hbm.1, s32[3,512]{1,0:T(4,128)} %bin_hbm.1), custom_call_target="tpu_custom_call" | custom-call | tf_op jit(solution)/shard_map/pallas_call | solution.py:155
  5.5 21.8 %all_to_all.15 = bf16[32,80,128]{2,1,0:T(8,128)(2,1)S(1)} all-to-all(bf16[32,80,128]{2,1,0:T(8,128)(2,1)S(1)} %shard_map.109), channel_id=1, replica_groups=mesh['b'=8,'a'=4,'chan'=8] {'a','chan'}, dimensions={0} | all-to-all | bytes 1310720 | tf_op jit(solution)/shard_map/all_to_all | solution.py:323
  27.3 0.0 copy-done.4
  27.3 5.2 %shard_map.110 = bf16[8,64,384]{2,1,0:T(8,128)(2,1)S(1)} custom-call(s32[3]{0:T(128)S(1)} %copy-done.4, bf16[4,8,80,128]{3,2,1,0:T(8,128)(2,1)S(1)} %bitcast.5), custom_call_target="tpu_custom_call" | custom-call | tf_op jit(solution)/shard_map/pallas_call | solution.py:253
  32.5 23.2 %all_to_all.16.part_ref = bf16[8,64,384]{2,1,0:T(8,128)(2,1)S(1)} all-to-all(bf16[8,64,384]{2,1,0:T(8,128)(2,1)S(1)} %shard_map.110), channel_id=1, replica_groups=mesh['b'=8,'a'=4,'chan'=8] {'b'}, dimensions={0} | all-to-all | bytes 786432 | tf_op jit(solution)/shard_map/all_to_all | solution.py:325
  55.7 0.1 shard_map.111
  55.7 11.7 %all_to_all.17 = bf16[32,8,384]{2,1,0:T(8,128)(2,1)S(1)} all-to-all(bf16[32,8,384]{2,1,0:T(8,128)(2,1)S(1)} %bitcast.7), channel_id=1, replica_groups=mesh['b'=8,'a'=4,'chan'=8] {'a','chan'}, dimensions={0} | all-to-all | bytes 393216 | tf_op jit(solution)/shard_map/all_to_all | solution.py:327
  67.5 0.0 copy-done.2
  67.5 0.0 copy-done.3
  67.5 0.0 copy-done
  67.5 0.0 copy-done.1
  67.5 0.9 %shard_map.112 = f32[3,128,128]{2,1,0:T(8,128)} custom-call(s32[1]{0:T(128)} %bitcast.place_ref, bf16[256,384]{1,0:T(8,128)(2,1)S(1)} %bitcast.6, f32[128,256]{1,0:T(8,128)S(1)} %copy-done.1, f32[128,256]{1,0:T(8,128)S(1)} %copy-done, f32[32,256]{1,0:T(8,128)S(1)} %copy-done.3, f32[32,256]{1,0:T(8,128)S(1)} %copy-done.2), custom_call_target="tpu_custom_call" | custom-call | tf_op jit(solution)/shard_map/pallas_call | solution.py:307
Async XLA Ops:
  0.0 67.5 %copy-start.2 = (f32[32,256]{1,0:T(8,128)S(1)}, f32[32,256]{1,0:T(8,128)}, u32[]{:S(2)}) copy-start(f32[32,256]{1,0:T(8,128)} %constant.26.clone.second_ref) | copy-start | bytes 98308
  0.0 67.5 %copy-start.3 = (f32[32,256]{1,0:T(8,128)S(1)}, f32[32,256]{1,0:T(8,128)}, u32[]{:S(2)}) copy-start(f32[32,256]{1,0:T(8,128)} %constant.25.clone.first_ref) | copy-start | bytes 98308
  0.0 67.5 %copy-start = (f32[128,256]{1,0:T(8,128)S(1)}, f32[128,256]{1,0:T(8,128)}, u32[]{:S(2)}) copy-start(f32[128,256]{1,0:T(8,128)} %constant.24.clone.sin_ref) | copy-start | bytes 393220
  0.0 67.5 %copy-start.1 = (f32[128,256]{1,0:T(8,128)S(1)}, f32[128,256]{1,0:T(8,128)}, u32[]{:S(2)}) copy-start(f32[128,256]{1,0:T(8,128)} %constant.23.clone.cos_ref) | copy-start | bytes 393220
  0.0 27.3 %copy-start.4 = (s32[3]{0:T(128)S(1)}, s32[3]{0:T(128)}, u32[]{:S(2)}) copy-start(s32[3]{0:T(128)} %block_ref.1) | copy-start | bytes 40
